TPU v7x, 256 devices: a whole 4x4x8 slice. The times are simulated.
256 devices in a mesh: dp: 2 (over x_lo), expert: 8 (over z), shard: 16 (over x_hi, y, core).
Axes of the slice: x: 4 (x_hi: 2, x_lo: 2; x = x_hi * 2 + x_lo), y: 4, z: 8, core: 2. Of those that a mesh axis runs over, the one named last changes fastest.
Arguments:
- tokens: bfloat16 [2048, 6144], P(('dp', 'expert', 'shard')), may hold values from -6 to 6
- gate_up_weight: bfloat16 [8, 2, 8192, 6144], P(None, None, ('dp', 'expert', 'shard')), may hold values from -0.078125 to 0.078125
- down_weight: bfloat16 [8, 8192, 6144], P(None, ('dp', 'expert', 'shard')), may hold values from -0.0625 to 0.0625
- expert_ids: int32 [2048, 2], P(('dp', 'expert', 'shard')), may hold values from 0 to 7, as said below
- slot_ids: int32 [2048, 2], P(('dp', 'expert', 'shard')), may hold values from 0 to 3, as said below
- gate_values: float32 [2048, 2], P(('dp', 'expert', 'shard')), may hold values from 0.1 to 1
- old_place: int32 [8], replicated, may hold values from 0 to 7, each once
- new_place: int32 [8], replicated, may hold values from 0 to 7, each once
Outputs:
- mixed_out: bfloat16 [2048, 6144], P(('dp', 'expert', 'shard'))
Inputs may be any that keep to these rules, and one draw needn't show every extreme that they name: `expert_ids`: each token names 2 different experts; among the 8 tokens of one block no expert is named more than 4 times, and one expert is named exactly 4 times in every block. `slot_ids`: within one block, two choices that name the same expert have different slots. `old_place`: each expert number appears once. `new_place`: each expert number appears once.
All inputs are finite; a program needn't handle non-finite values.
Results may differ from a plain program's by a relative error of at most 0.02.
Values may be sent and summed in bfloat16 or wider, within the bound.
A program may use at most 128 MiB of HBM per device.

v0:
```python
import jax
import jax.numpy as jnp
from jax import lax
from jax.sharding import PartitionSpec as P


def placement_order(old_place, new_place):
    slot_total = old_place.shape[0]
    matches = (new_place[:, None] == old_place[None, :]).astype(jnp.int32)
    return jnp.sum(matches * jnp.arange(slot_total, dtype=jnp.int32)[None, :], axis=1)


def swiglu_rows(row_block, pair_weight):
    gate_up = jnp.einsum("rd,gud->rgu", row_block, pair_weight, preferred_element_type=jnp.float32)
    return (jax.nn.silu(gate_up[:, 0]) * gate_up[:, 1]).astype(jnp.bfloat16)


def local(
    tokens, gate_up_weight, down_weight, expert_ids, slot_ids, gate_values, old_place, new_place
):
    experts = gate_up_weight.shape[0]
    sliver = gate_up_weight.shape[2]
    model_width = tokens.shape[1]
    tok_rows = tokens.shape[0]
    choices_per_token = expert_ids.shape[1]
    capacity = 2 * tok_rows * choices_per_token // experts
    cell_count = experts * capacity
    data_ways = lax.axis_size("dp")
    slot_order = placement_order(old_place, new_place)
    cell_ids = expert_ids * capacity + slot_ids
    cell_range = jnp.arange(cell_count, dtype=jnp.int32)
    cell_hits = (cell_ids[:, :, None] == cell_range[None, None, :]).astype(jnp.float32)
    token_picks = jnp.sum(cell_hits, axis=1)
    dispatched = jnp.dot(
        token_picks.T.astype(jnp.bfloat16), tokens, preferred_element_type=jnp.float32
    ).astype(jnp.bfloat16)
    received = lax.all_to_all(
        dispatched.reshape(experts, capacity, model_width),
        "expert",
        split_axis=0,
        concat_axis=0,
        tiled=True,
    )
    own_rows = received.reshape(cell_count, model_width)
    sectioned_in = gate_up_weight.reshape(experts, 2, data_ways, sliver // data_ways, model_width)
    sectioned_down = down_weight.reshape(experts, 1, data_ways, sliver // data_ways, model_width)
    sectioned_in = jnp.take(sectioned_in, slot_order, axis=0)
    sectioned_down = jnp.take(sectioned_down, slot_order, axis=0)
    relaid_in, relaid_down = (
        lax.all_to_all(
            lax.all_to_all(sectioned_in, "dp", split_axis=2, concat_axis=3, tiled=True),
            "expert",
            split_axis=0,
            concat_axis=3,
            tiled=True,
        ),
        lax.all_to_all(
            lax.all_to_all(sectioned_down, "dp", split_axis=2, concat_axis=3, tiled=True),
            "expert",
            split_axis=0,
            concat_axis=3,
            tiled=True,
        ),
    )
    full_in, full_down = (
        lax.all_gather(relaid_in, "dp", axis=3, tiled=True),
        lax.all_gather(relaid_down, "dp", axis=3, tiled=True),
    )
    pair_in = full_in.reshape(2, -1, model_width)
    pair_down = full_down.reshape(-1, model_width)
    group_rows = lax.all_gather(own_rows, "shard", axis=0, tiled=True)
    summed = lax.psum_scatter(
        jnp.dot(
            swiglu_rows(group_rows, pair_in), pair_down, preferred_element_type=jnp.float32
        ).astype(jnp.bfloat16),
        "shard",
        scatter_dimension=0,
        tiled=True,
    )
    returned = lax.all_to_all(
        summed.reshape(experts, capacity, model_width),
        "expert",
        split_axis=0,
        concat_axis=0,
        tiled=True,
    )
    combine_weights = jnp.sum(cell_hits * gate_values[:, :, None], axis=1)
    mixed_out = jnp.dot(
        combine_weights,
        returned.reshape(cell_count, model_width).astype(jnp.float32),
        precision=lax.Precision.HIGHEST,
    )
    return mixed_out.astype(jnp.bfloat16)


def solution(mesh):
    in_specs = (
        P(("dp", "expert", "shard"), None),
        P(None, None, ("dp", "expert", "shard"), None),
        P(None, ("dp", "expert", "shard"), None),
        P(("dp", "expert", "shard"), None),
        P(("dp", "expert", "shard"), None),
        P(("dp", "expert", "shard"), None),
        P(),
        P(),
    )
    out_specs = P(("dp", "expert", "shard"), None)
    return jax.shard_map(local, mesh=mesh, in_specs=in_specs, out_specs=out_specs, check_vma=False)
```

profile of v0, /device:TPU:8, one launch (start us, length us, event | category | flops | bytes accessed | tf_op | source)
XLA Modules:
  0.0 681.6 jit_solution(10519561180992360223)
XLA Ops:
  6.5 0.0 copy-start
  6.5 0.8 multiply_add_fusion
  7.4 0.9 convert_reduce_fusion
  8.3 1.2 convolution_convert_fusion.1
  9.5 0.9 reshape.64
  10.4 8.5 %all-to-all-start = ((bf16[8,4,6144]{2,1,0:T(4,128)(2,1)}), bf16[8,4,6144]{2,1,0:T(4,128)(2,1)S(1)}, u32[]{:S(2)}, u32[]{:S(2)}) async-start(bf16[8,4,6144]{2,1,0:T(4,128)(2,1)} %reshape.64), calls=%async_computation | async-start | bytes 786432 | tf_op jit(solution)/shard_map/all_to_all | solution.py:37
  18.8 0.9 select_reduce_fusion.1
  19.7 6.4 gather_fusion
  26.1 3.5 broadcast_select_fusion
  29.6 3.1 copy.24
  32.6 0.9 all-to-all-done
  33.5 6.3 all-to-all-start.1
  39.8 0.0 all-gather.4.cloned.1.call-start
  39.9 0.9 reshape.65
  40.7 0.0 all-gather.4.cloned.1.call-update
  40.8 0.0 all-gather.6.cloned.1.call-start
  40.8 89.5 %all-to-all-done.1 = bf16[8,2,2,16,6144]{4,3,1,0,2:T(8,128)(2,1)} async-done(((bf16[8,2,2,16,6144]{4,3,1,0,2:T(8,128)(2,1)}), bf16[8,2,2,16,6144]{4,3,1,0,2:T(8,128)(2,1)}, u32[]{:S(2)}, u32[]{:S(2)}) %all-to-all-start.1) | async-done | bytes 6291488 | tf_op jit(solution)/shard_map/all_to_all | solution.py:51
  130.3 3.5 copy.25
  133.8 145.8 %all_to_all.64 = bf16[8,2,1,32,6144]{4,3,1,2,0:T(8,128)(2,1)S(1)} all-to-all(bf16[8,2,1,32,6144]{4,3,1,2,0:T(8,128)(2,1)S(1)} %bitcast.37), channel_id=1, replica_groups=mesh['dp'=2,'expert'=8,'shard'=16] {'expert'}, dimensions={0} | all-to-all | bytes 12582912 | tf_op jit(solution)/shard_map/all_to_all | solution.py:50
  279.7 3.1 copy.27
  282.8 0.0 all-gather.6.cloned.1.call-update
  282.8 0.0 all-gather.8.cloned.1.call-start
  282.8 0.0 copy-done
  282.8 2.4 gather_fusion.1
  285.3 2.3 bitcast_select_fusion
  287.5 0.3 copy.28
  287.9 63.1 %all_to_all.65 = bf16[8,1,2,16,6144]{4,3,0,1,2:T(8,128)(2,1)S(1)} all-to-all(bf16[8,1,2,16,6144]{4,3,0,1,2:T(8,128)(2,1)S(1)} %copy.28), channel_id=1, replica_groups=mesh['dp'=2,'expert'=8,'shard'=16] {'dp'}, dimensions={2} | all-to-all | bytes 6291456 | tf_op jit(solution)/shard_map/all_to_all | solution.py:58
  350.9 0.3 copy.29
  351.2 66.1 %all_to_all.66 = bf16[8,1,1,32,6144]{4,3,2,1,0:T(8,128)(2,1)} all-to-all(bf16[8,1,1,32,6144]{4,3,2,1,0:T(8,128)(2,1)S(1)} %bitcast.40), channel_id=1, replica_groups=mesh['dp'=2,'expert'=8,'shard'=16] {'expert'}, dimensions={0} | all-to-all | bytes 6291456 | tf_op jit(solution)/shard_map/all_to_all | solution.py:57
  417.4 0.0 all-gather.8.cloned.1.call-update
  417.4 0.0 reduce-scatter.2.cloned.1.call-start
  417.5 0.0 all-gather.4.cloned.1.call-done
  417.5 41.2 %all-gather.6.cloned.1.call-done = bf16[1,2,1,512,6144]{4,3,1,2,0:T(8,128)(2,1)} async-done(((bf16[1,2,1,256,6144]{4,3,1,2,0:T(8,128)(2,1)}), bf16[1,2,1,512,6144]{4,3,1,2,0:T(8,128)(2,1)}) %all-gather.6.cloned.1.call-update) | async-done | bytes 12582928 | tf_op jit(solution)/shard_map/all_gather | solution.py:66
  458.6 12.5 %fusion = f32[512,2,512]{2,0,1:T(8,128)} fusion(bf16[1,2,1,512,6144]{4,3,1,2,0:T(8,128)(2,1)} %all-gather.6.cloned.1.call-done, bf16[512,6144]{1,0:T(8,128)(2,1)} %all-gather.4.cloned.1.call-done), kind=kOutput, calls=%fused_computation.2 | convolution fusion | flops 6442450944 | bytes 20971520 | tf_op jit(solution)/shard_map/rd,gud->rgu/dot_general | solution.py:14
  471.2 72.6 %all-gather.8.cloned.1.call-done = bf16[1,1,1,512,6144]{4,3,2,1,0:T(8,128)(2,1)} async-done(((bf16[1,1,1,256,6144]{4,3,2,1,0:T(8,128)(2,1)}), bf16[1,1,1,512,6144]{4,3,2,1,0:T(8,128)(2,1)}) %all-gather.8.cloned.1.call-update) | async-done | bytes 6291472 | tf_op jit(solution)/shard_map/all_gather | solution.py:67
  543.8 0.0 copy-start.1
  543.8 9.7 %convolution_convert_fusion = bf16[512,6144]{1,0:T(8,128)(2,1)} fusion(bf16[1,1,1,512,6144]{4,3,2,1,0:T(8,128)(2,1)} %all-gather.8.cloned.1.call-done, f32[512,2,512]{2,0,1:T(8,128)} %fusion), kind=kOutput, calls=%fused_computation.4 | convolution fusion | flops 3225944064 | bytes 14680064 | tf_op jit(solution)/shard_map/dot_general | solution.py:73
  553.5 0.0 reduce-scatter.2.cloned.1.call-update
  553.6 98.3 %reduce-scatter.2.cloned.1.call-done = bf16[32,6144]{1,0:T(8,128)(2,1)} async-done(((bf16[512,6144]{1,0:T(8,128)(2,1)}), bf16[32,6144]{1,0:T(8,128)(2,1)}) %reduce-scatter.2.cloned.1.call-update) | async-done | bytes 393232 | tf_op jit(solution)/shard_map/reduce_scatter | solution.py:72
  651.9 1.1 reshape.70
  653.0 20.0 %all_to_all.67 = bf16[8,4,6144]{2,1,0:T(4,128)(2,1)} all-to-all(bf16[8,4,6144]{2,1,0:T(4,128)(2,1)S(1)} %reshape.70), channel_id=1, replica_groups=mesh['dp'=2,'expert'=8,'shard'=16] {'expert'}, dimensions={0} | all-to-all | bytes 786432 | tf_op jit(solution)/shard_map/all_to_all | solution.py:80
  673.1 1.1 reshape.71
  674.1 0.9 convolution_convert_fusion.2
  675.1 0.0 copy-done.1
  (3 shorter events, 0.0 us)
Async XLA Ops:
  6.5 276.3 %copy-start = (bf16[8,32,6144]{2,1,0:T(8,128)(2,1)S(1)}, bf16[8,32,6144]{2,1,0:T(8,128)(2,1)}, u32[]{:S(2)}) copy-start(bf16[8,32,6144]{2,1,0:T(8,128)(2,1)} %param.10) | copy-start | bytes 9437188
  10.4 23.2 %all-to-all-start = ((bf16[8,4,6144]{2,1,0:T(4,128)(2,1)}), bf16[8,4,6144]{2,1,0:T(4,128)(2,1)S(1)}, u32[]{:S(2)}, u32[]{:S(2)}) async-start(bf16[8,4,6144]{2,1,0:T(4,128)(2,1)} %reshape.64), calls=%async_computation | async-start | bytes 786432 | tf_op jit(solution)/shard_map/all_to_all | solution.py:37
  33.5 96.8 %all-to-all-start.1 = ((bf16[8,2,2,16,6144]{4,3,1,0,2:T(8,128)(2,1)}), bf16[8,2,2,16,6144]{4,3,1,0,2:T(8,128)(2,1)}, u32[]{:S(2)}, u32[]{:S(2)}) async-start(bf16[8,2,2,16,6144]{4,3,1,0,2:T(8,128)(2,1)} %copy.24), calls=%async_computation.1 | async-start | bytes 12582912 | tf_op jit(solution)/shard_map/all_to_all | solution.py:51
  39.8 377.6 %all-gather.4.cloned.1.call-start = ((), (), s32[]{:S(2)}) async-start(), calls=%async_computation.7 | async-start | bytes 6684672 | tf_op jit(solution)/shard_map/all_gather | solution.py:71
  40.8 417.9 %all-gather.6.cloned.1.call-start = ((), (), s32[]{:S(2)}) async-start(), calls=%async_computation.8 | async-start | bytes 18874368 | tf_op jit(solution)/shard_map/all_gather | solution.py:66
  282.8 261.0 %all-gather.8.cloned.1.call-start = ((), (), s32[]{:S(2)}) async-start(), calls=%async_computation.9 | async-start | bytes 9437184 | tf_op jit(solution)/shard_map/all_gather | solution.py:67
  417.4 234.5 %reduce-scatter.2.cloned.1.call-start = ((), (), s32[]{:S(2)}) async-start(), calls=%async_computation.10 | async-start | bytes 6684672 | tf_op jit(solution)/shard_map/reduce_scatter | solution.py:72
  543.8 131.2 %copy-start.1 = (bf16[8,32,6144]{2,1,0:T(8,128)(2,1)S(1)}, bf16[8,32,6144]{2,1,0:T(8,128)(2,1)}, u32[]{:S(2)}) copy-start(bf16[8,32,6144]{2,1,0:T(8,128)(2,1)} %param.10) | copy-start | bytes 9437188
Sparse Core Ops, SparseCore 0:
  43.4 90.1 all-gather.3
  282.9 175.6 all-gather.5
  460.4 83.3 all-gather.7
  553.7 98.1 reduce-scatter.1
where the time goes:
time: 682 us
  waiting for transfers between devices  303 us (44%)
  blocking collectives  295 us (43%)
  matrix products  24.3 us (4%)
  local copies, waits for them, and re-layouts  23.1 us (3%)
  starting transfers between devices  15 us (2%)
  between operations  13.2 us (2%)
  other arithmetic  8.31 us (1%)
    all_to_all x1, blocking collectives, local(): lax.all_to_all(lax.all_to_all(sectioned_in, 'dp', split_axis=2, concat_ax...  146 us
    reduce_scatter x1, waiting for transfers between devices, local(): lax.psum_scatter(jnp.dot(swiglu_rows(group_rows, pair_in), pair_down, pre...  98.3 us
    all_to_all x1, waiting for transfers between devices, local(): lax.all_to_all(sectioned_in, 'dp', split_axis=2, concat_axis=3, tiled=True)  89.5 us
    all_gather x1, waiting for transfers between devices, local(): lax.all_gather(relaid_down, 'dp', axis=3, tiled=True)  72.6 us
    all_to_all x1, blocking collectives, local(): lax.all_to_all(lax.all_to_all(sectioned_down, 'dp', split_axis=2, concat_...  66.1 us
    all_to_all x1, blocking collectives, local(): lax.all_to_all(sectioned_down, 'dp', split_axis=2, concat_axis=3, tiled=T...  63.1 us
    all_gather x1, waiting for transfers between devices, local(): lax.all_gather(relaid_in, 'dp', axis=3, tiled=True)  41.2 us
    all_to_all x1, blocking collectives, local(): lax.all_to_all(summed.reshape(experts, capacity, model_width), 'expert',...  20 us
  transfers between devices with their start and end apart: 6, of which 5 were waited for; matrix products, arithmetic and copies ran while one was open for 6% of the time, Pallas kernels for 0%

commit v1 on v0

v1 whole, which is shorter than its diff:
```python
import functools
import heapq

import jax
import jax.numpy as jnp
from jax import lax
from jax.experimental import pallas as pl
from jax.experimental.pallas import tpu as pltpu
from jax.sharding import PartitionSpec as P

AXES = ("dp", "expert", "shard")
ROWS = 8
WIDE = 2048
EXTRA = 128
SLOTS = 8
SLIVER = 32
UNITS = 2 * SLOTS * SLIVER
RING = {"x": 4, "y": 4, "z": 8}
ORDER = (("x", "y", "z"), ("z", "y", "x"), ("z", "x", "y"))
RATE, LATENCY = 44500.0, 1.8


class Message:
    def __init__(self, part, stage, dist, sign, sub):
        self.part, self.stage, self.dist, self.sign, self.sub = part, stage, dist, sign, sub
        self.key = (part, stage, dist, sign, sub)
        self.axis = ORDER[part][stage]
        self.link = (self.axis, sign)


def subs_of(part, stage):
    n1, n2 = RING[ORDER[part][0]], RING[ORDER[part][1]]
    if stage == 0:
        return [(0, 0, 1)]
    if stage == 1:
        return [(0, 0, n1 // 2), (0, n1 // 2, n1 // 2)]
    return [(i2, i1, 4) for i2 in range(n2) for i1 in range(0, n1, 4)]


def messages():
    out = []
    for part in range(3):
        for stage in range(3):
            size = RING[ORDER[part][stage]]
            subs = subs_of(part, stage)
            for dist in range(1, size // 2 + 1):
                for sign in (1, -1):
                    for sub in range(len(subs)):
                        if dist == size // 2:
                            if len(subs) == 1:
                                if sign != (-1 if part == 2 else 1):
                                    continue
                            elif (sub < len(subs) // 2) != (sign == 1):
                                continue
                        out.append(Message(part, stage, dist, sign, sub))
    return out


def blocks_of(msg, ring_index):
    i2, i1, n = subs_of(msg.part, msg.stage)[msg.sub]
    size = RING[msg.axis]
    r = ring_index % size
    if msg.stage == 0:
        return [(0, 0, r)]
    if msg.stage == 1:
        return [(0, r, i1 + j) for j in range(n)]
    return [(r, i2, i1 + j) for j in range(n)]


def simulate(sends, recv_needs, jobs, recv_cost, timers=()):
    done, issued, order = set(), set(), []
    link_free, arrivals = {}, []
    now = 0.0
    ready = []
    jobs = list(jobs)

    def issue():
        for key, (msg, size, needs) in sends.items():
            if key not in issued and needs <= done:
                issued.add(key)
                order.append(("send", key))
                start = max(now, link_free.get(msg.link, 0.0))
                link_free[msg.link] = start + size / RATE
                heapq.heappush(arrivals, (start + size / RATE + LATENCY, key))

    issue()
    timers = list(timers)
    total = len(sends)
    handled = 0
    while handled < total or jobs:
        while timers and timers[0][0] <= now:
            token = timers.pop(0)[1]
            order.append(("job", token))
            done.add(token)
        while arrivals and arrivals[0][0] <= now:
            ready.append(heapq.heappop(arrivals))
        pick = next((r for r in ready if recv_needs[r[1]] <= done), None)
        if pick is not None:
            ready.remove(pick)
            now += recv_cost
            order.append(("recv", pick[1]))
            done.add(("recv",) + pick[1])
            handled += 1
            issue()
            continue
        job = next((j for j in jobs if j[2] <= done), None)
        if job is not None:
            jobs.remove(job)
            now += job[1]
            order.append(("job", job[0]))
            done.add(job[0])
            issue()
            continue
        now = max(now, min([arrivals[0][0]] + [t[0] for t in timers]))
    return order, now


def gather_order():
    msgs = messages()
    source = {}
    for m in msgs:
        for b in blocks_of(m, -m.dist * m.sign):
            source[(m.part,) + b] = ("recv",) + m.key
    sends = {}
    for m in msgs:
        src = blocks_of(m, -(m.dist - 1) * m.sign)
        needs = {source[(m.part,) + b] for b in src if (m.part,) + b in source}
        width = WIDE + (EXTRA if m.part == 0 else 0)
        sends[m.key] = (m, len(src) * ROWS * width * 2, needs)
    jobs = []

    def slab_needs(part, i3s):
        return {v for k, v in source.items() if k[0] == part and k[1] in i3s}

    for part, slabs in GATE_UP_JOBS:
        needs = slab_needs(part, slabs) | {("weights",)}
        jobs.append((("up", part, slabs), 1.0 * len(slabs) if part == 0 else 2.0, needs))
    return sends, simulate(sends, {m.key: set() for m in msgs}, jobs, 0.1, [(22.0, ("weights",))])


GATE_UP_JOBS = (
    (0, (0,)), (1, (0,)), (2, (0,)), (0, (1, 7)), (1, (1,)), (1, (3,)), (2, (1,)), (2, (3,)),
    (0, (2, 6)), (0, (3, 5)), (1, (2,)), (2, (2,)), (0, (4,)),
)
DOWN_JOBS = (
    (0, (4,)), (1, (2,)), (2, (2,)), (0, (3, 5)), (1, (1,)), (2, (1,)), (1, (3,)), (2, (3,)),
    (0, (2, 6)), (0, (1, 7)), (1, (0,)), (2, (0,)), (0, (0,)),
)


def scatter_order():
    msgs = messages()
    by_key = {m.key: m for m in msgs}
    job_of = {}
    for part, slabs in DOWN_JOBS:
        for i3 in slabs:
            job_of[(part, i3)] = ("down", part, slabs)
    adds = {}
    for m in msgs:
        for b in blocks_of(m, (m.dist - 1) * m.sign):
            adds.setdefault((m.part,) + b, []).append(m)
    sends, recv_needs = {}, {}
    for m in msgs:
        src = blocks_of(m, m.dist * m.sign)
        needs = set()
        for b in src:
            needs.add(job_of[(m.part, b[0])])
            for a in adds.get((m.part,) + b, []):
                if a.stage > m.stage or (a.stage == m.stage and a.sign == m.sign and a.dist == m.dist + 1):
                    needs.add(("recv",) + a.key)
        sends[m.key] = (m, len(src) * ROWS * WIDE * 2, needs)
        recv_needs[m.key] = {job_of[(m.part, b[0])] for b in blocks_of(m, (m.dist - 1) * m.sign)}
    jobs = []
    for part, slabs in DOWN_JOBS:
        jobs.append((("down", part, slabs), 0.5 * len(slabs) if part == 0 else 1.0, set()))
    return sends, simulate(sends, recv_needs, jobs, 0.2)


def device_at(x, y, z, core):
    x, y, z = lax.rem(x + 4, 4), lax.rem(y + 4, 4), lax.rem(z + 8, 8)
    return (lax.rem(x, 2), z, (x // 2) * 8 + y * 2 + core)


def kernel(
    tok_ref, gu_ref, dn_ref, ids_ref, gv_ref, old_ref, new_ref, out_ref,
    tok0, tok1, tok2, w_gu, w_dn, acc, hid, xs, hs,
    l30, l20, l10, l31, l21, l11, l32, l22, l12,
    own_sem, w_send, w_recv, ag_send, ag_recv, rs_send, rs_recv,
):
    toks = (tok0, tok1, tok2)
    lands = ((l10, l20, l30), (l11, l21, l31), (l12, l22, l32))
    dp, z, shard = (lax.axis_index(a) for a in AXES)
    core, y, x = lax.rem(shard, 2), lax.rem(shard // 2, 4), (shard // 8) * 2 + dp
    partner = device_at(x, y, z, 1 - core)
    near = {
        ("x", 1): device_at(x + 1, y, z, core), ("x", -1): device_at(x - 1, y, z, core),
        ("y", 1): device_at(x, y + 1, z, core), ("y", -1): device_at(x, y - 1, z, core),
        ("z", 1): device_at(x, y, z + 1, core), ("z", -1): device_at(x, y, z - 1, core),
    }
    mesh_id = pl.DeviceIdType.MESH
    barrier = pltpu.get_barrier_semaphore()
    for dev in (partner, *near.values()):
        pl.semaphore_signal(barrier, inc=1, device_id=dev, device_id_type=mesh_id)

    own = [
        pltpu.make_async_copy(tok_ref.at[:, pl.ds(p * WIDE, WIDE)], toks[p].at[0, 0, 0, :, pl.ds(0, WIDE)], own_sem.at[p])
        for p in range(3)
    ]
    for copy in own:
        copy.start()
    own_w = [
        pltpu.make_async_copy(gu_ref.at[:, 0], w_gu.at[0, 0], own_sem.at[3]),
        pltpu.make_async_copy(gu_ref.at[:, 1], w_gu.at[1, 0], own_sem.at[4]),
        pltpu.make_async_copy(dn_ref, w_dn.at[0], own_sem.at[5]),
    ]
    for copy in own_w:
        copy.start()

    lane = lax.broadcasted_iota(jnp.int32, (ROWS, EXTRA), 1)
    slot = lax.rem(lane, SLOTS)
    held = jnp.zeros((ROWS, EXTRA), jnp.int32)
    for j in range(SLOTS):
        held = jnp.where(slot == j, old_ref[j], held)
    weight = jnp.zeros((ROWS, EXTRA), jnp.float32)
    for k in range(2):
        ids = jnp.broadcast_to(ids_ref[:, k : k + 1], (ROWS, EXTRA))
        gate = jnp.broadcast_to(gv_ref[:, k : k + 1], (ROWS, EXTRA))
        place = jnp.zeros((ROWS, EXTRA), jnp.int32)
        for e in range(SLOTS):
            place = jnp.where(ids == e, new_ref[e], place)
        weight = weight + jnp.where(place == held, gate, 0.0)
    high = weight.astype(jnp.bfloat16).astype(jnp.float32)
    coded = jnp.where(lane < SLOTS, high, jnp.where(lane < 2 * SLOTS, weight - high, 0.0))
    tok0[0, 0, 0, :, WIDE:] = coded.astype(jnp.bfloat16)

    for copy in own:
        copy.wait()
    pl.semaphore_wait(barrier, 7)

    def remote(src, dst, send, recv, dev):
        return pltpu.make_async_remote_copy(
            src_ref=src, dst_ref=dst, send_sem=send, recv_sem=recv, device_id=dev, device_id_type=mesh_id
        )

    def view(msg, ring_index, narrow):
        i3, i2, i1 = blocks_of(msg, ring_index)[0]
        n = subs_of(msg.part, msg.stage)[msg.sub][2]
        ref = toks[msg.part]
        if narrow and msg.part == 0:
            return ref.at[i3, i2, pl.ds(i1, n), :, pl.ds(0, WIDE)]
        return ref.at[i3, i2, pl.ds(i1, n)]

    ag_sends, (ag_order, _) = gather_order()
    index = {key: i for i, key in enumerate(ag_sends)}
    gathers = {}
    for key, (m, _, _) in ag_sends.items():
        gathers[key] = remote(
            view(m, -(m.dist - 1) * m.sign, False), view(m, -m.dist * m.sign, False),
            ag_send.at[index[key]], ag_recv.at[index[key]], near[m.link],
        )
    crossing = [
        remote(gu_ref.at[:, 0], w_gu.at[0, 1], w_send.at[0], w_recv.at[0], partner),
        remote(gu_ref.at[:, 1], w_gu.at[1, 1], w_send.at[1], w_recv.at[1], partner),
        remote(dn_ref, w_dn.at[1], w_send.at[2], w_recv.at[2], partner),
    ]

    def gate_up(part, slabs):
        ref = toks[part]
        for j, i3 in enumerate(slabs):
            n2, n1 = ref.shape[1], ref.shape[2]
            rows = n1 * ROWS
            base = j * n2 * rows

            @pl.loop(0, n2)
            def _(i2):
                block = ref[i3, i2, :, :, pl.ds(0, WIDE)].astype(jnp.float32)
                start = pl.multiple_of(base + i2 * rows, 16)
                xs[pl.ds(start, rows), :] = block.reshape(rows, WIDE).astype(jnp.bfloat16)

        total = 128 * len(slabs) if part == 0 else 256

        @pl.loop(0, 4)
        def _(n):
            half, group = n // 2, lax.rem(n, 2)
            right = w_gu[half, group, :, :, pl.ds(part * WIDE, WIDE)].reshape(SLOTS * SLIVER, WIDE)
            prod = lax.dot_general(
                xs[0:total, :], right, (((1,), (1,)), ((), ())), preferred_element_type=jnp.float32
            )
            cols = pl.ds(pl.multiple_of(n * 256, 256), 256)
            if part == 0:
                for j, i3 in enumerate(slabs):
                    acc[i3, :, :, :, cols] += prod[j * 128 : (j + 1) * 128].reshape(4, 4, ROWS, 256)
            else:
                for i2 in range(4):
                    where = (i2, slabs[0]) if part == 1 else (slabs[0], i2)
                    acc[:, where[0], where[1], :, cols] += prod[i2 * 64 : (i2 + 1) * 64].reshape(8, ROWS, 256)

    crossed = False
    for kind, what in ag_order:
        if kind != "send" and not crossed:
            crossed = True
            for copy in crossing:
                copy.start()
        if kind == "send":
            gathers[what].start()
        elif kind == "recv":
            gathers[what].wait_recv()
        elif what == ("weights",):
            acc[...] = jnp.zeros_like(acc)
            for copy in own_w + crossing:
                copy.wait()
        else:
            gate_up(what[1], what[2])
    for copy in gathers.values():
        copy.wait_send()

    code_row = lax.broadcasted_iota(jnp.int32, (EXTRA, UNITS), 0)
    unit_slot = lax.rem(lax.broadcasted_iota(jnp.int32, (EXTRA, UNITS), 1) // SLIVER, SLOTS)
    spread = jnp.where((code_row < 2 * SLOTS) & (lax.rem(code_row, SLOTS) == unit_slot), 1.0, 0.0)
    spread = spread.astype(jnp.bfloat16)

    @pl.loop(0, 8)
    def _(i3):
        code = tok0[i3, :, :, :, pl.ds(WIDE, EXTRA)].astype(jnp.float32).reshape(128, EXTRA)
        scale = jnp.dot(code.astype(jnp.bfloat16), spread, preferred_element_type=jnp.float32)
        gate = acc[i3, :, :, :, pl.ds(0, UNITS)].reshape(128, UNITS)
        up = acc[i3, :, :, :, pl.ds(UNITS, UNITS)].reshape(128, UNITS)
        value = gate / (1.0 + jnp.exp(-gate)) * up * scale
        hid[i3] = value.reshape(4, 4, ROWS, UNITS)

    def down(part, slabs):
        total = 128 * len(slabs) if part == 0 else 256
        if part == 0:
            for j, i3 in enumerate(slabs):
                hs[j * 128 : (j + 1) * 128, :] = hid[i3].reshape(128, UNITS).astype(jnp.bfloat16)
        else:
            for i2 in range(4):
                where = (i2, slabs[0]) if part == 1 else (slabs[0], i2)
                rows = hid[:, where[0], where[1]].reshape(64, UNITS)
                hs[i2 * 64 : (i2 + 1) * 64, :] = rows.astype(jnp.bfloat16)

        @pl.loop(0, WIDE // 256)
        def _(n):
            cols = pl.ds(pl.multiple_of(part * WIDE + n * 256, 256), 256)
            right = w_dn[:, :, :, cols].reshape(UNITS, 256)
            prod = jnp.dot(hs[0:total, :], right, preferred_element_type=jnp.float32)
            cols = pl.ds(pl.multiple_of(n * 256, 256), 256)
            ref = toks[part]
            n2, n1 = ref.shape[1], ref.shape[2]
            for j, i3 in enumerate(slabs):
                piece = prod[j * 128 : (j + 1) * 128] if part == 0 else prod
                ref[i3, :, :, :, cols] = piece.reshape(n2, n1, ROWS, 256).astype(jnp.bfloat16)

    rs_sends, (rs_order, _) = scatter_order()

    def landing(m):
        return lands[m.part][m.stage].at[0 if m.sign == 1 else 1, m.dist - 1, m.sub]

    scatters = {}
    for key, (m, _, _) in rs_sends.items():
        scatters[key] = remote(
            view(m, m.dist * m.sign, True), landing(m),
            rs_send.at[index[key]], rs_recv.at[index[key]], near[m.link],
        )
    for kind, what in rs_order:
        if kind == "send":
            scatters[what].start()
        elif kind == "job":
            down(what[1], what[2])
        else:
            m = rs_sends[what][0]
            scatters[what].wait_recv()
            target = view(m, (m.dist - 1) * m.sign, True)
            target[...] = target[...] + landing(m)[...]
    for p in range(3):
        out_ref[:, p * WIDE : (p + 1) * WIDE] = toks[p][0, 0, 0, :, 0:WIDE]
    for copy in scatters.values():
        copy.wait_send()


def local(
    tokens, gate_up_weight, down_weight, expert_ids, slot_ids, gate_values, old_place, new_place
):
    count = len(messages())
    bf16, f32 = jnp.bfloat16, jnp.float32
    any_space = pl.BlockSpec(memory_space=pl.ANY)
    vmem = pl.BlockSpec(memory_space=pltpu.VMEM)
    smem = pl.BlockSpec(memory_space=pltpu.SMEM)
    lands = []
    for part in range(3):
        for stage in (2, 1, 0):
            subs = subs_of(part, stage)
            ring = RING[ORDER[part][stage]]
            lands.append(pltpu.VMEM((2, ring // 2, len(subs), subs[0][2], ROWS, WIDE), bf16))
    return pl.pallas_call(
        kernel,
        out_shape=jax.ShapeDtypeStruct((ROWS, 3 * WIDE), bf16),
        in_specs=[any_space, any_space, any_space, vmem, vmem, smem, smem],
        out_specs=vmem,
        scratch_shapes=[
            pltpu.VMEM((8, 4, 4, ROWS, WIDE + EXTRA), bf16),
            pltpu.VMEM((4, 4, 8, ROWS, WIDE), bf16),
            pltpu.VMEM((4, 4, 8, ROWS, WIDE), bf16),
            pltpu.VMEM((2, 2, SLOTS, SLIVER, 3 * WIDE), bf16),
            pltpu.VMEM((2, SLOTS, SLIVER, 3 * WIDE), bf16),
            pltpu.VMEM((8, 4, 4, ROWS, 2 * UNITS), f32),
            pltpu.VMEM((8, 4, 4, ROWS, UNITS), f32),
            pltpu.VMEM((256, WIDE), bf16),
            pltpu.VMEM((256, UNITS), bf16),
            *lands,
            pltpu.SemaphoreType.DMA((6,)),
            pltpu.SemaphoreType.DMA((3,)),
            pltpu.SemaphoreType.DMA((3,)),
            pltpu.SemaphoreType.DMA((count,)),
            pltpu.SemaphoreType.DMA((count,)),
            pltpu.SemaphoreType.DMA((count,)),
            pltpu.SemaphoreType.DMA((count,)),
        ],
        compiler_params=pltpu.CompilerParams(
            collective_id=0, has_side_effects=True, vmem_limit_bytes=67043328
        ),
        name="expert_layer",
    )(tokens, gate_up_weight, down_weight, expert_ids, gate_values, old_place, new_place)


def solution(mesh):
    in_specs = (
        P(AXES, None),
        P(None, None, AXES, None),
        P(None, AXES, None),
        P(AXES, None),
        P(AXES, None),
        P(AXES, None),
        P(),
        P(),
    )
    out_specs = P(AXES, None)
    return jax.shard_map(local, mesh=mesh, in_specs=in_specs, out_specs=out_specs, check_vma=False)
```

time: 682 us -> 148 us (0.22)
  waiting for transfers between devices: 303 us -> 0 us
  blocking collectives: 295 us -> 0 us
  Pallas kernels: 0 us -> 144 us
  matrix products: 24.3 us -> 0 us
  local copies, waits for them, and re-layouts: 23.1 us -> 4.23 us
  starting transfers between devices: 15 us -> 0 us
  between operations: 13.2 us -> 0.01 us
  other arithmetic: 8.31 us -> 0 us
    all_to_all x4 -> x0, blocking collectives: 295 us -> none  [the longest x1 146 us: local(): lax.all_to_all(lax.all_to_all(sectioned_in, 'dp', split_axis=2, concat_ax...]
    pallas_call x0 -> x1, Pallas kernels: none -> 144 us  [local(): pl.pallas_call(kernel, out_shape=jax.ShapeDtypeStruct((ROWS, 3 * WIDE), b...]
    all_gather x3 -> x0, waiting for transfers between devices: 114 us -> none  [the longest x1 72.6 us: local(): lax.all_gather(relaid_down, 'dp', axis=3, tiled=True)]
    reduce_scatter x1 -> x0, waiting for transfers between devices: 98.3 us -> none  [local(): lax.psum_scatter(jnp.dot(swiglu_rows(group_rows, pair_in), pair_down, pre...]
    all_to_all x2 -> x0, waiting for transfers between devices: 90.4 us -> none  [the longest x1 89.5 us: local(): lax.all_to_all(sectioned_in, 'dp', split_axis=2, concat_axis=3, tiled=True)]
    dot_general x4 -> x0, matrix products: 24.3 us -> none  [the longest x1 12.5 us: swiglu_rows(): jnp.einsum('rd,gud->rgu', row_block, pair_weight, preferred_element_type=...]
    all_to_all x2 -> x0, starting transfers between devices: 14.8 us -> none  [the longest x1 8.47 us: local(): lax.all_to_all(dispatched.reshape(experts, capacity, model_width), 'exper...]
    gather x2 -> x0, local copies, waits for them, and re-layouts: 8.81 us -> none  [the longest x1 6.39 us: local(): sectioned_in = jnp.take(sectioned_in, slot_order, axis=0)]
  transfers between devices with their start and end apart: 6 -> 0, of which waited for: 5 -> 0; matrix products, arithmetic and copies ran while one was open for 6% -> 0% of each run, Pallas kernels for 0% -> 0%
where the time goes in v1:
time: 148 us
  Pallas kernels  144 us (97%)
  local copies, waits for them, and re-layouts  4.23 us (3%)
    pallas_call x1, Pallas kernels, local(): pl.pallas_call(kernel, out_shape=jax.ShapeDtypeStruct((ROWS, 3 * WIDE), b...  144 us
    unnamed x3, local copies, waits for them, and re-layouts  4.23 us

profile of v1, /device:TPU:8, one launch (start us, length us, event | category | flops | bytes accessed | tf_op | source)
XLA Modules:
  0.0 147.8 jit_solution(9109051310521044957)
XLA Ops:
  0.0 1.3 copy.8.ids_ref
  1.3 1.3 copy.9.gv_ref
  2.7 143.5 %expert_layer.1 = bf16[8,6144]{1,0:T(8,128)(2,1)} custom-call(bf16[8,6144]{1,0:T(8,128)(2,1)} %tok_ref.1, bf16[8,2,32,6144]{3,2,1,0:T(8,128)(2,1)} %gu_ref.1, bf16[8,32,6144]{2,1,0:T(8,128)(2,1)} %dn_ref.1, s32[8,2]{1,0:T(8,128)} %copy.8.ids_ref, f32[8,2]{1,0:T(8,128)} %copy.9.gv_ref, s32[8]{0:T(128)} %old_ref.1, s32[8]{0:T(128)} %new_ref.1), custom_call_target="tpu_custom_call" | custom-call | tf_op jit(solution)/shard_map/expert_layer/pallas_call | solution.py:395
  146.2 1.5 %copy.11 = bf16[8,6144]{1,0:T(8,128)(2,1)} copy(bf16[8,6144]{1,0:T(8,128)(2,1)} %expert_layer.1) | data formatting | bytes 196608

commit v2 on v1

--- a/solution.py
+++ b/solution.py
@@ -18,6 +18,7 @@
 RING = {"x": 4, "y": 4, "z": 8}
 ORDER = (("x", "y", "z"), ("z", "y", "x"), ("z", "x", "y"))
 RATE, LATENCY = 44500.0, 1.8
+AHEAD = 3.0
 
 
 class Message:
@@ -28,13 +29,33 @@
         self.link = (self.axis, sign)
 
 
+def position(ring_index, size):
+    r = ring_index % size
+    return 0 if r == 0 else (2 * r - 1 if r <= size // 2 else 2 * (size - r))
+
+
+def groups(n1):
+    return [(0, 1), (1, 2), (3, 1)] if n1 == 4 else [(0, 1), (1, 2), (3, 2), (5, 3)]
+
+
 def subs_of(part, stage):
     n1, n2 = RING[ORDER[part][0]], RING[ORDER[part][1]]
     if stage == 0:
         return [(0, 0, 1)]
+    first = [(0, i1, n) for i1, n in groups(n1)]
     if stage == 1:
-        return [(0, 0, n1 // 2), (0, n1 // 2, n1 // 2)]
-    return [(i2, i1, 4) for i2 in range(n2) for i1 in range(0, n1, 4)]
+        return first
+    rest = [(0, 4)] if n1 == 4 else [(0, 3), (3, 5)]
+    return first + [(i2, i1, n) for i2 in range(1, n2) for i1, n in rest]
+
+
+def far_sign(part, stage, sub):
+    subs = subs_of(part, stage)
+    if stage == 0:
+        return -1 if part == 2 else 1
+    if stage == 1:
+        return 1 if sub in (0, len(subs) - 1) else -1
+    return 1 if subs[sub][0] in (0, 3) else -1
 
 
 def messages():
@@ -42,76 +63,93 @@
     for part in range(3):
         for stage in range(3):
             size = RING[ORDER[part][stage]]
-            subs = subs_of(part, stage)
             for dist in range(1, size // 2 + 1):
                 for sign in (1, -1):
-                    for sub in range(len(subs)):
-                        if dist == size // 2:
-                            if len(subs) == 1:
-                                if sign != (-1 if part == 2 else 1):
-                                    continue
-                            elif (sub < len(subs) // 2) != (sign == 1):
-                                continue
-                        out.append(Message(part, stage, dist, sign, sub))
+                    for sub in range(len(subs_of(part, stage))):
+                        if dist < size // 2 or far_sign(part, stage, sub) == sign:
+                            out.append(Message(part, stage, dist, sign, sub))
     return out
 
 
 def blocks_of(msg, ring_index):
     i2, i1, n = subs_of(msg.part, msg.stage)[msg.sub]
-    size = RING[msg.axis]
-    r = ring_index % size
+    p = position(ring_index, RING[msg.axis])
     if msg.stage == 0:
-        return [(0, 0, r)]
+        return [(0, 0, p)]
     if msg.stage == 1:
-        return [(0, r, i1 + j) for j in range(n)]
-    return [(r, i2, i1 + j) for j in range(n)]
-
-
-def simulate(sends, recv_needs, jobs, recv_cost, timers=()):
-    done, issued, order = set(), set(), []
-    link_free, arrivals = {}, []
+        return [(0, p, i1 + j) for j in range(n)]
+    return [(p, i2, i1 + j) for j in range(n)]
+
+
+def simulate(sends, recv_needs, jobs, recv_cost, timers=(), ahead=AHEAD):
+    readers = {}
+    for key, (_, _, needs) in sends.items():
+        for token in needs:
+            readers.setdefault(token, []).append(key)
+    tails = {}
+
+    def tail(key):
+        if key not in tails:
+            after = max((tail(k) for k in readers.get(("recv",) + key, [])), default=0.0)
+            tails[key] = sends[key][1] / RATE + LATENCY + after
+        return tails[key]
+
+    number = {key: i for i, key in enumerate(sends)}
+    missing = {key: len(needs) for key, (_, _, needs) in sends.items()}
+    queues, link_free, arrivals = {}, {}, []
+    done, order, ready = set(), [], []
     now = 0.0
-    ready = []
-    jobs = list(jobs)
+
+    def offer(key):
+        heapq.heappush(queues.setdefault(sends[key][0].link, []), (-tail(key), number[key], key))
+
+    def finish(token):
+        done.add(token)
+        for key in readers.get(token, []):
+            missing[key] -= 1
+            if not missing[key]:
+                offer(key)
 
     def issue():
-        for key, (msg, size, needs) in sends.items():
-            if key not in issued and needs <= done:
-                issued.add(key)
+        for link, queue in queues.items():
+            while queue and link_free.get(link, 0.0) - now < ahead:
+                key = heapq.heappop(queue)[2]
                 order.append(("send", key))
-                start = max(now, link_free.get(msg.link, 0.0))
-                link_free[msg.link] = start + size / RATE
-                heapq.heappush(arrivals, (start + size / RATE + LATENCY, key))
-
+                sent = max(now, link_free.get(link, 0.0)) + sends[key][1] / RATE
+                link_free[link] = sent
+                heapq.heappush(arrivals, (sent + LATENCY, key))
+
+    for key, count in missing.items():
+        if not count:
+            offer(key)
+    jobs, timers = list(jobs), list(timers)
+    handled = 0
     issue()
-    timers = list(timers)
-    total = len(sends)
-    handled = 0
-    while handled < total or jobs:
+    while handled < len(sends) or jobs:
         while timers and timers[0][0] <= now:
             token = timers.pop(0)[1]
             order.append(("job", token))
-            done.add(token)
+            finish(token)
         while arrivals and arrivals[0][0] <= now:
             ready.append(heapq.heappop(arrivals))
         pick = next((r for r in ready if recv_needs[r[1]] <= done), None)
+        job = next((j for j in jobs if j[2] <= done), None)
         if pick is not None:
             ready.remove(pick)
             now += recv_cost
             order.append(("recv", pick[1]))
-            done.add(("recv",) + pick[1])
+            finish(("recv",) + pick[1])
             handled += 1
-            issue()
-            continue
-        job = next((j for j in jobs if j[2] <= done), None)
-        if job is not None:
+        elif job is not None:
             jobs.remove(job)
             now += job[1]
             order.append(("job", job[0]))
-            done.add(job[0])
-            issue()
-            continue
-        now = max(now, min([arrivals[0][0]] + [t[0] for t in timers]))
+            finish(job[0])
+        else:
+            times = [a[0] for a in arrivals[:1]] + [t[0] for t in timers[:1]]
+            times += [free - ahead + 0.01 for link, free in link_free.items() if queues.get(link)]
+            now = max(now, min(times))
+        issue()
     return order, now
 
 
@@ -128,33 +166,32 @@
         width = WIDE + (EXTRA if m.part == 0 else 0)
         sends[m.key] = (m, len(src) * ROWS * width * 2, needs)
     jobs = []
-
-    def slab_needs(part, i3s):
-        return {v for k, v in source.items() if k[0] == part and k[1] in i3s}
-
-    for part, slabs in GATE_UP_JOBS:
-        needs = slab_needs(part, slabs) | {("weights",)}
-        jobs.append((("up", part, slabs), 1.0 * len(slabs) if part == 0 else 2.0, needs))
+    for part, slabs, low, high in GATE_UP_JOBS:
+        needs = {v for k, v in source.items() if k[0] == part and k[1] in slabs and low <= k[2] < high}
+        rows = (32 if part == 0 else 64) * (high - low) * len(slabs)
+        jobs.append((("up", part, slabs, low, high), UP_COST[rows], needs | {("weights",)}))
     return sends, simulate(sends, {m.key: set() for m in msgs}, jobs, 0.1, [(22.0, ("weights",))])
 
 
+UP_COST = {128: 1.3, 256: 2.0}
 GATE_UP_JOBS = (
-    (0, (0,)), (1, (0,)), (2, (0,)), (0, (1, 7)), (1, (1,)), (1, (3,)), (2, (1,)), (2, (3,)),
-    (0, (2, 6)), (0, (3, 5)), (1, (2,)), (2, (2,)), (0, (4,)),
+    (0, (0,), 0, 4), (1, (0,), 0, 4), (2, (0,), 0, 4), (0, (1, 2), 0, 4), (1, (1,), 0, 4),
+    (2, (1,), 0, 4), (1, (2,), 0, 4), (2, (2,), 0, 4), (0, (3, 4), 0, 4), (0, (5, 6), 0, 4),
+    (1, (3,), 0, 2), (2, (3,), 0, 2), (1, (3,), 2, 4), (2, (3,), 2, 4), (0, (7,), 0, 4),
 )
 DOWN_JOBS = (
-    (0, (4,)), (1, (2,)), (2, (2,)), (0, (3, 5)), (1, (1,)), (2, (1,)), (1, (3,)), (2, (3,)),
-    (0, (2, 6)), (0, (1, 7)), (1, (0,)), (2, (0,)), (0, (0,)),
+    ("hid", 0), (0, (7,)), ("hid", 1), (1, (3,)), ("hid", 2), (2, (3,)), ("hid", 3), (0, (5, 6)),
+    (1, (1,)), (2, (1,)), (1, (2,)), (2, (2,)), (0, (3, 4)), (0, (1, 2)), (1, (0,)), (2, (0,)), (0, (0,)),
 )
 
 
 def scatter_order():
-    msgs = messages()
-    by_key = {m.key: m for m in msgs}
+    msgs = messages()[::-1]
     job_of = {}
     for part, slabs in DOWN_JOBS:
-        for i3 in slabs:
-            job_of[(part, i3)] = ("down", part, slabs)
+        if part != "hid":
+            for i3 in slabs:
+                job_of[(part, i3)] = ("down", part, slabs)
     adds = {}
     for m in msgs:
         for b in blocks_of(m, (m.dist - 1) * m.sign):
@@ -172,7 +209,10 @@
         recv_needs[m.key] = {job_of[(m.part, b[0])] for b in blocks_of(m, (m.dist - 1) * m.sign)}
     jobs = []
     for part, slabs in DOWN_JOBS:
-        jobs.append((("down", part, slabs), 0.5 * len(slabs) if part == 0 else 1.0, set()))
+        if part == "hid":
+            jobs.append((("hid", slabs), 0.6, set()))
+        else:
+            jobs.append((("down", part, slabs), 0.6 * len(slabs) if part == 0 else 1.2, set()))
     return sends, simulate(sends, recv_needs, jobs, 0.2)
 
 
@@ -183,7 +223,7 @@
 
 def kernel(
     tok_ref, gu_ref, dn_ref, ids_ref, gv_ref, old_ref, new_ref, out_ref,
-    tok0, tok1, tok2, w_gu, w_dn, acc, hid, xs, hs,
+    tok0, tok1, tok2, w_gu, w_dn, acc, scale, spread, xs, hs,
     l30, l20, l10, l31, l21, l11, l32, l22, l12,
     own_sem, w_send, w_recv, ag_send, ag_recv, rs_send, rs_recv,
 ):
@@ -218,13 +258,19 @@
 
     lane = lax.broadcasted_iota(jnp.int32, (ROWS, EXTRA), 1)
     slot = lax.rem(lane, SLOTS)
+    diagonal = lax.broadcasted_iota(jnp.int32, (ROWS, ROWS), 0) == lax.broadcasted_iota(jnp.int32, (ROWS, ROWS), 1)
+
+    def column(ref, k):
+        row = jnp.broadcast_to(ref[k : k + 1, :], (ROWS, ROWS))
+        return jnp.sum(jnp.where(diagonal, row, jnp.zeros_like(row)), axis=1, keepdims=True)
+
     held = jnp.zeros((ROWS, EXTRA), jnp.int32)
     for j in range(SLOTS):
         held = jnp.where(slot == j, old_ref[j], held)
     weight = jnp.zeros((ROWS, EXTRA), jnp.float32)
     for k in range(2):
-        ids = jnp.broadcast_to(ids_ref[:, k : k + 1], (ROWS, EXTRA))
-        gate = jnp.broadcast_to(gv_ref[:, k : k + 1], (ROWS, EXTRA))
+        ids = jnp.broadcast_to(column(ids_ref, k), (ROWS, EXTRA))
+        gate = jnp.broadcast_to(column(gv_ref, k), (ROWS, EXTRA))
         place = jnp.zeros((ROWS, EXTRA), jnp.int32)
         for e in range(SLOTS):
             place = jnp.where(ids == e, new_ref[e], place)
@@ -264,20 +310,18 @@
         remote(dn_ref, w_dn.at[1], w_send.at[2], w_recv.at[2], partner),
     ]
 
-    def gate_up(part, slabs):
+    def gate_up(part, slabs, low, high):
         ref = toks[part]
+        count, rows = high - low, ref.shape[2] * ROWS
         for j, i3 in enumerate(slabs):
-            n2, n1 = ref.shape[1], ref.shape[2]
-            rows = n1 * ROWS
-            base = j * n2 * rows
-
-            @pl.loop(0, n2)
+
+            @pl.loop(0, count)
             def _(i2):
-                block = ref[i3, i2, :, :, pl.ds(0, WIDE)].astype(jnp.float32)
-                start = pl.multiple_of(base + i2 * rows, 16)
+                block = ref[i3, low + i2, :, :, pl.ds(0, WIDE)].astype(jnp.float32)
+                start = pl.multiple_of((j * count + i2) * rows, 16)
                 xs[pl.ds(start, rows), :] = block.reshape(rows, WIDE).astype(jnp.bfloat16)
 
-        total = 128 * len(slabs) if part == 0 else 256
+        total = count * rows * len(slabs)
 
         @pl.loop(0, 4)
         def _(n):
@@ -291,9 +335,15 @@
                 for j, i3 in enumerate(slabs):
                     acc[i3, :, :, :, cols] += prod[j * 128 : (j + 1) * 128].reshape(4, 4, ROWS, 256)
             else:
-                for i2 in range(4):
-                    where = (i2, slabs[0]) if part == 1 else (slabs[0], i2)
+                for i2 in range(count):
+                    where = (low + i2, slabs[0]) if part == 1 else (slabs[0], low + i2)
                     acc[:, where[0], where[1], :, cols] += prod[i2 * 64 : (i2 + 1) * 64].reshape(8, ROWS, 256)
+
+        if part == 0:
+            for i3 in slabs:
+                code = tok0[i3, :, :, :, pl.ds(WIDE, EXTRA)].astype(jnp.float32).reshape(128, EXTRA)
+                wide = jnp.dot(code.astype(jnp.bfloat16), spread[...], preferred_element_type=jnp.float32)
+                scale[i3] = wide.reshape(4, 4, ROWS, UNITS)
 
     crossed = False
     for kind, what in ag_order:
@@ -307,36 +357,43 @@
             gathers[what].wait_recv()
         elif what == ("weights",):
             acc[...] = jnp.zeros_like(acc)
+            code_row = lax.broadcasted_iota(jnp.int32, (EXTRA, UNITS), 0)
+            unit_slot = lax.rem(lax.broadcasted_iota(jnp.int32, (EXTRA, UNITS), 1) // SLIVER, SLOTS)
+            chosen = (code_row < 2 * SLOTS) & (lax.rem(code_row, SLOTS) == unit_slot)
+            spread[...] = jnp.where(chosen, 1.0, 0.0).astype(jnp.bfloat16)
             for copy in own_w + crossing:
                 copy.wait()
         else:
-            gate_up(what[1], what[2])
+            gate_up(*what[1:])
     for copy in gathers.values():
         copy.wait_send()
 
-    code_row = lax.broadcasted_iota(jnp.int32, (EXTRA, UNITS), 0)
-    unit_slot = lax.rem(lax.broadcasted_iota(jnp.int32, (EXTRA, UNITS), 1) // SLIVER, SLOTS)
-    spread = jnp.where((code_row < 2 * SLOTS) & (lax.rem(code_row, SLOTS) == unit_slot), 1.0, 0.0)
-    spread = spread.astype(jnp.bfloat16)
-
-    @pl.loop(0, 8)
-    def _(i3):
-        code = tok0[i3, :, :, :, pl.ds(WIDE, EXTRA)].astype(jnp.float32).reshape(128, EXTRA)
-        scale = jnp.dot(code.astype(jnp.bfloat16), spread, preferred_element_type=jnp.float32)
-        gate = acc[i3, :, :, :, pl.ds(0, UNITS)].reshape(128, UNITS)
-        up = acc[i3, :, :, :, pl.ds(UNITS, UNITS)].reshape(128, UNITS)
-        value = gate / (1.0 + jnp.exp(-gate)) * up * scale
-        hid[i3] = value.reshape(4, 4, ROWS, UNITS)
+    def hidden(where):
+        gate = acc[(*where, slice(None), pl.ds(0, UNITS))]
+        up = acc[(*where, slice(None), pl.ds(UNITS, UNITS))]
+        acc[(*where, slice(None), pl.ds(0, UNITS))] = (
+            gate / (1.0 + jnp.exp(-gate)) * up * scale[(*where, slice(None), slice(None))]
+        )
+
+    def hidden_rows(step):
+        if step == 0:
+            pl.loop(0, 4)(lambda i: hidden((7, i, slice(None))))
+        elif step == 1:
+            pl.loop(0, 7)(lambda i: hidden((i, slice(None), 3)))
+        elif step == 2:
+            pl.loop(0, 7)(lambda i: hidden((i, 3, pl.ds(0, 3))))
+        else:
+            pl.loop(0, 21)(lambda i: hidden((i // 3, lax.rem(i, 3), pl.ds(0, 3))))
 
     def down(part, slabs):
         total = 128 * len(slabs) if part == 0 else 256
         if part == 0:
             for j, i3 in enumerate(slabs):
-                hs[j * 128 : (j + 1) * 128, :] = hid[i3].reshape(128, UNITS).astype(jnp.bfloat16)
+                hs[j * 128 : (j + 1) * 128, :] = acc[i3, :, :, :, pl.ds(0, UNITS)].reshape(128, UNITS).astype(jnp.bfloat16)
         else:
             for i2 in range(4):
                 where = (i2, slabs[0]) if part == 1 else (slabs[0], i2)
-                rows = hid[:, where[0], where[1]].reshape(64, UNITS)
+                rows = acc[:, where[0], where[1], :, pl.ds(0, UNITS)].reshape(64, UNITS)
                 hs[i2 * 64 : (i2 + 1) * 64, :] = rows.astype(jnp.bfloat16)
 
         @pl.loop(0, WIDE // 256)
@@ -354,7 +411,8 @@
     rs_sends, (rs_order, _) = scatter_order()
 
     def landing(m):
-        return lands[m.part][m.stage].at[0 if m.sign == 1 else 1, m.dist - 1, m.sub]
+        i2, i1, n = subs_of(m.part, m.stage)[m.sub]
+        return lands[m.part][m.stage].at[0 if m.sign == 1 else 1, m.dist - 1, i2, pl.ds(i1, n)]
 
     scatters = {}
     for key, (m, _, _) in rs_sends.items():
@@ -365,6 +423,8 @@
     for kind, what in rs_order:
         if kind == "send":
             scatters[what].start()
+        elif kind == "job" and what[0] == "hid":
+            hidden_rows(what[1])
         elif kind == "job":
             down(what[1], what[2])
         else:
@@ -389,9 +449,10 @@
     lands = []
     for part in range(3):
         for stage in (2, 1, 0):
-            subs = subs_of(part, stage)
+            n1, n2, _ = (RING[axis] for axis in ORDER[part])
             ring = RING[ORDER[part][stage]]
-            lands.append(pltpu.VMEM((2, ring // 2, len(subs), subs[0][2], ROWS, WIDE), bf16))
+            shape = (n2 if stage == 2 else 1, n1 if stage else 1)
+            lands.append(pltpu.VMEM((2, ring // 2, *shape, ROWS, WIDE), bf16))
     return pl.pallas_call(
         kernel,
         out_shape=jax.ShapeDtypeStruct((ROWS, 3 * WIDE), bf16),
@@ -405,6 +466,7 @@
             pltpu.VMEM((2, SLOTS, SLIVER, 3 * WIDE), bf16),
             pltpu.VMEM((8, 4, 4, ROWS, 2 * UNITS), f32),
             pltpu.VMEM((8, 4, 4, ROWS, UNITS), f32),
+            pltpu.VMEM((EXTRA, UNITS), bf16),
             pltpu.VMEM((256, WIDE), bf16),
             pltpu.VMEM((256, UNITS), bf16),
             *lands,
@@ -420,7 +482,7 @@
             collective_id=0, has_side_effects=True, vmem_limit_bytes=67043328
         ),
         name="expert_layer",
-    )(tokens, gate_up_weight, down_weight, expert_ids, gate_values, old_place, new_place)
+    )(tokens, gate_up_weight, down_weight, expert_ids.T, gate_values.T, old_place, new_place)
 
 
 def solution(mesh):

time: 148 us -> 138 us (0.932)
  Pallas kernels: 144 us -> 135 us
  local copies, waits for them, and re-layouts: 4.23 us -> 1.54 us
    pallas_call x1, Pallas kernels: 144 us -> 135 us  [local(): pl.pallas_call(kernel, out_shape=jax.ShapeDtypeStruct((ROWS, 3 * WIDE), b...]
    unnamed x3 -> x1, local copies, waits for them, and re-layouts: 4.23 us -> 1.54 us
where the time goes in v2:
time: 138 us; the launch traced here: 137 us
  Pallas kernels  135 us (98%)
  local copies, waits for them, and re-layouts  1.54 us (1%)
    pallas_call x1, Pallas kernels, local(): pl.pallas_call(kernel, out_shape=jax.ShapeDtypeStruct((ROWS, 3 * WIDE), b...  135 us

profile of v2, /device:TPU:8, one launch (start us, length us, event | category | flops | bytes accessed | tf_op | source)
XLA Modules:
  0.0 136.5 jit_solution(358681004315485731)
XLA Ops:
  0.0 135.0 %expert_layer.1 = bf16[8,6144]{1,0:T(8,128)(2,1)} custom-call(bf16[8,6144]{1,0:T(8,128)(2,1)} %tok_ref.1, bf16[8,2,32,6144]{3,2,1,0:T(8,128)(2,1)} %gu_ref.1, bf16[8,32,6144]{2,1,0:T(8,128)(2,1)} %dn_ref.1, s32[2,8]{1,0:T(2,128)} %bitcast.2, f32[2,8]{1,0:T(2,128)} %bitcast.3, s32[8]{0:T(128)} %old_ref.1, s32[8]{0:T(128)} %new_ref.1), custom_call_target="tpu_custom_call" | custom-call | tf_op jit(solution)/shard_map/expert_layer/pallas_call | solution.py:456
  135.0 1.5 %copy.9 = bf16[8,6144]{1,0:T(8,128)(2,1)} copy(bf16[8,6144]{1,0:T(8,128)(2,1)} %expert_layer.1) | data formatting | bytes 196608

commit v3 on v2

--- a/solution.py
+++ b/solution.py
@@ -19,6 +19,8 @@
 ORDER = (("x", "y", "z"), ("z", "y", "x"), ("z", "x", "y"))
 RATE, LATENCY = 44500.0, 1.8
 AHEAD = 3.0
+GATHER_BONUS = {(2, 1): 2.1, (2, 2): 8.3, (1, 1): 12.7, (0, 2): 9.2, (0, 0): 12.6, (0, 1): -0.2, (1, 2): 11.2, (1, 0): 5.2, (2, 0): 5.8}
+SCATTER_BONUS = {(0, 0): -6.3, (2, 0): 13.8, (1, 0): 10.2, (1, 1): 9.9, (1, 2): -3.4, (0, 1): -1.4, (2, 1): -2.5, (0, 2): 5.3, (2, 2): -1.7}
 
 
 class Message:
@@ -81,7 +83,7 @@
     return [(p, i2, i1 + j) for j in range(n)]
 
 
-def simulate(sends, recv_needs, jobs, recv_cost, timers=(), ahead=AHEAD):
+def simulate(sends, recv_needs, jobs, recv_cost, timers=(), ahead=AHEAD, bonus=None):
     readers = {}
     for key, (_, _, needs) in sends.items():
         for token in needs:
@@ -101,7 +103,8 @@
     now = 0.0
 
     def offer(key):
-        heapq.heappush(queues.setdefault(sends[key][0].link, []), (-tail(key), number[key], key))
+        rank = tail(key) + (bonus or {}).get(key[:2], 0.0)
+        heapq.heappush(queues.setdefault(sends[key][0].link, []), (-rank, number[key], key))
 
     def finish(token):
         done.add(token)
@@ -166,22 +169,41 @@
         width = WIDE + (EXTRA if m.part == 0 else 0)
         sends[m.key] = (m, len(src) * ROWS * width * 2, needs)
     jobs = []
-    for part, slabs, low, high in GATE_UP_JOBS:
-        needs = {v for k, v in source.items() if k[0] == part and k[1] in slabs and low <= k[2] < high}
-        rows = (32 if part == 0 else 64) * (high - low) * len(slabs)
-        jobs.append((("up", part, slabs, low, high), UP_COST[rows], needs | {("weights",)}))
-    return sends, simulate(sends, {m.key: set() for m in msgs}, jobs, 0.1, [(22.0, ("weights",))])
-
-
-UP_COST = {128: 1.3, 256: 2.0}
+    for part, slabs, i2s, held in GATE_UP_JOBS:
+        needs = {v for k, v in source.items() if k[0] == part and k[1] in slabs and k[2] in i2s}
+        rows = (32 if part == 0 else 64) * len(i2s) * len(slabs)
+        cost = UP_COST[rows] * len(held)
+        jobs.append((("up", part, slabs, i2s, held), cost, needs | {("weights", held[-1])}))
+    timers = [(OWN_AT, ("weights", 0)), (PARTNER_AT, ("weights", 1))]
+    return sends, simulate(sends, {m.key: set() for m in msgs}, jobs, 0.1, timers, bonus=GATHER_BONUS)
+
+
+OWN_AT, PARTNER_AT = 5.0, 20.0
+UP_COST = {64: 0.75, 128: 0.8, 192: 0.85, 256: 0.9, 384: 1.3}
+HIDDEN_COST = (0.8, 0.4, 0.7, 1.5)
+ALL = (0, 1, 2, 3)
 GATE_UP_JOBS = (
-    (0, (0,), 0, 4), (1, (0,), 0, 4), (2, (0,), 0, 4), (0, (1, 2), 0, 4), (1, (1,), 0, 4),
-    (2, (1,), 0, 4), (1, (2,), 0, 4), (2, (2,), 0, 4), (0, (3, 4), 0, 4), (0, (5, 6), 0, 4),
-    (1, (3,), 0, 2), (2, (3,), 0, 2), (1, (3,), 2, 4), (2, (3,), 2, 4), (0, (7,), 0, 4),
+    (1, (3,), ALL, (0, 1)),
+    (1, (1,), (0,), (0, 1)),
+    (0, (7,), ALL, (0, 1)),
+    (0, (0, 1, 2), ALL, (0, 1)),
+    (1, (2,), (1, 2, 3), (0, 1)),
+    (1, (2,), (0,), (0, 1)),
+    (2, (0,), ALL, (0, 1)),
+    (1, (0,), (2, 3), (0, 1)),
+    (2, (2,), ALL, (0, 1)),
+    (1, (0,), (0, 1), (0, 1)),
+    (2, (1,), (0, 1), (0, 1)),
+    (2, (1,), (2, 3), (0, 1)),
+    (2, (3,), ALL, (0, 1)),
+    (1, (1,), (1, 2, 3), (0, 1)),
+    (0, (3, 4), ALL, (0, 1)),
+    (0, (5, 6), ALL, (0, 1)),
 )
 DOWN_JOBS = (
-    ("hid", 0), (0, (7,)), ("hid", 1), (1, (3,)), ("hid", 2), (2, (3,)), ("hid", 3), (0, (5, 6)),
-    (1, (1,)), (2, (1,)), (1, (2,)), (2, (2,)), (0, (3, 4)), (0, (1, 2)), (1, (0,)), (2, (0,)), (0, (0,)),
+    ("hid", 0), (2, (3,)), ("hid", 1), (0, (7,)), ("hid", 2), (1, (3,)),
+    ("hid", 3), (0, (5, 6)), (1, (1,)), (2, (1,)), (2, (2,)), (0, (3, 4)),
+    (1, (2,)), (2, (0,)), (0, (0,)), (1, (0,)), (0, (1, 2)),
 )
 
 
@@ -210,10 +232,10 @@
     jobs = []
     for part, slabs in DOWN_JOBS:
         if part == "hid":
-            jobs.append((("hid", slabs), 0.6, set()))
+            jobs.append((("hid", slabs), HIDDEN_COST[slabs], set()))
         else:
-            jobs.append((("down", part, slabs), 0.6 * len(slabs) if part == 0 else 1.2, set()))
-    return sends, simulate(sends, recv_needs, jobs, 0.2)
+            jobs.append((("down", part, slabs), 0.75 * len(slabs) if part == 0 else 1.1, set()))
+    return sends, simulate(sends, recv_needs, jobs, 0.2, bonus=SCATTER_BONUS)
 
 
 def device_at(x, y, z, core):
@@ -250,7 +272,7 @@
         copy.start()
     own_w = [
         pltpu.make_async_copy(gu_ref.at[:, 0], w_gu.at[0, 0], own_sem.at[3]),
-        pltpu.make_async_copy(gu_ref.at[:, 1], w_gu.at[1, 0], own_sem.at[4]),
+        pltpu.make_async_copy(gu_ref.at[:, 1], w_gu.at[0, 1], own_sem.at[4]),
         pltpu.make_async_copy(dn_ref, w_dn.at[0], own_sem.at[5]),
     ]
     for copy in own_w:
@@ -305,41 +327,41 @@
             ag_send.at[index[key]], ag_recv.at[index[key]], near[m.link],
         )
     crossing = [
-        remote(gu_ref.at[:, 0], w_gu.at[0, 1], w_send.at[0], w_recv.at[0], partner),
+        remote(gu_ref.at[:, 0], w_gu.at[1, 0], w_send.at[0], w_recv.at[0], partner),
         remote(gu_ref.at[:, 1], w_gu.at[1, 1], w_send.at[1], w_recv.at[1], partner),
         remote(dn_ref, w_dn.at[1], w_send.at[2], w_recv.at[2], partner),
     ]
 
-    def gate_up(part, slabs, low, high):
+    def gate_up(part, slabs, i2s, held):
         ref = toks[part]
-        count, rows = high - low, ref.shape[2] * ROWS
+        count, rows = len(i2s), ref.shape[2] * ROWS
+        step = i2s[1] - i2s[0] if count > 1 else 1
         for j, i3 in enumerate(slabs):
 
             @pl.loop(0, count)
             def _(i2):
-                block = ref[i3, low + i2, :, :, pl.ds(0, WIDE)].astype(jnp.float32)
+                block = ref[i3, i2s[0] + step * i2, :, :, pl.ds(0, WIDE)].astype(jnp.float32)
                 start = pl.multiple_of((j * count + i2) * rows, 16)
                 xs[pl.ds(start, rows), :] = block.reshape(rows, WIDE).astype(jnp.bfloat16)
 
         total = count * rows * len(slabs)
 
-        @pl.loop(0, 4)
-        def _(n):
-            half, group = n // 2, lax.rem(n, 2)
-            right = w_gu[half, group, :, :, pl.ds(part * WIDE, WIDE)].reshape(SLOTS * SLIVER, WIDE)
+        @pl.loop(held[0], held[-1] + 1)
+        def _(group):
+            right = w_gu[group, :, :, :, pl.ds(part * WIDE, WIDE)].reshape(UNITS, WIDE)
             prod = lax.dot_general(
                 xs[0:total, :], right, (((1,), (1,)), ((), ())), preferred_element_type=jnp.float32
             )
-            cols = pl.ds(pl.multiple_of(n * 256, 256), 256)
+            cols = pl.ds(pl.multiple_of(group * UNITS, UNITS), UNITS)
             if part == 0:
                 for j, i3 in enumerate(slabs):
-                    acc[i3, :, :, :, cols] += prod[j * 128 : (j + 1) * 128].reshape(4, 4, ROWS, 256)
+                    acc[i3, :, :, :, cols] += prod[j * 128 : (j + 1) * 128].reshape(4, 4, ROWS, UNITS)
             else:
                 for i2 in range(count):
-                    where = (low + i2, slabs[0]) if part == 1 else (slabs[0], low + i2)
-                    acc[:, where[0], where[1], :, cols] += prod[i2 * 64 : (i2 + 1) * 64].reshape(8, ROWS, 256)
-
-        if part == 0:
+                    where = (i2s[i2], slabs[0]) if part == 1 else (slabs[0], i2s[i2])
+                    acc[:, where[0], where[1], :, cols] += prod[i2 * 64 : (i2 + 1) * 64].reshape(8, ROWS, UNITS)
+
+        if part == 0 and held[-1] == 1:
             for i3 in slabs:
                 code = tok0[i3, :, :, :, pl.ds(WIDE, EXTRA)].astype(jnp.float32).reshape(128, EXTRA)
                 wide = jnp.dot(code.astype(jnp.bfloat16), spread[...], preferred_element_type=jnp.float32)
@@ -351,17 +373,20 @@
             crossed = True
             for copy in crossing:
                 copy.start()
-        if kind == "send":
-            gathers[what].start()
-        elif kind == "recv":
-            gathers[what].wait_recv()
-        elif what == ("weights",):
             acc[...] = jnp.zeros_like(acc)
             code_row = lax.broadcasted_iota(jnp.int32, (EXTRA, UNITS), 0)
             unit_slot = lax.rem(lax.broadcasted_iota(jnp.int32, (EXTRA, UNITS), 1) // SLIVER, SLOTS)
             chosen = (code_row < 2 * SLOTS) & (lax.rem(code_row, SLOTS) == unit_slot)
             spread[...] = jnp.where(chosen, 1.0, 0.0).astype(jnp.bfloat16)
-            for copy in own_w + crossing:
+        if kind == "send":
+            gathers[what].start()
+        elif kind == "recv":
+            gathers[what].wait_recv()
+        elif what == ("weights", 1):
+            for copy in crossing:
+                copy.wait()
+        elif what == ("weights", 0):
+            for copy in own_w:
                 copy.wait()
         else:
             gate_up(*what[1:])
@@ -369,19 +394,23 @@
         copy.wait_send()
 
     def hidden(where):
-        gate = acc[(*where, slice(None), pl.ds(0, UNITS))]
-        up = acc[(*where, slice(None), pl.ds(UNITS, UNITS))]
-        acc[(*where, slice(None), pl.ds(0, UNITS))] = (
-            gate / (1.0 + jnp.exp(-gate)) * up * scale[(*where, slice(None), slice(None))]
-        )
+        width = UNITS // 2
+        values = []
+        for group in range(2):
+            gate = acc[(*where, slice(None), pl.ds(group * UNITS, width))]
+            up = acc[(*where, slice(None), pl.ds(group * UNITS + width, width))]
+            share = scale[(*where, slice(None), pl.ds(group * width, width))]
+            values.append(gate / (1.0 + jnp.exp(-gate)) * up * share)
+        for group in range(2):
+            acc[(*where, slice(None), pl.ds(group * width, width))] = values[group]
 
     def hidden_rows(step):
         if step == 0:
-            pl.loop(0, 4)(lambda i: hidden((7, i, slice(None))))
+            pl.loop(0, 8)(lambda i: hidden((i, 3, slice(None))))
         elif step == 1:
-            pl.loop(0, 7)(lambda i: hidden((i, slice(None), 3)))
+            pl.loop(0, 3)(lambda i: hidden((7, i, slice(None))))
         elif step == 2:
-            pl.loop(0, 7)(lambda i: hidden((i, 3, pl.ds(0, 3))))
+            pl.loop(0, 7)(lambda i: hidden((i, pl.ds(0, 3), 3)))
         else:
             pl.loop(0, 21)(lambda i: hidden((i // 3, lax.rem(i, 3), pl.ds(0, 3))))
 
@@ -396,17 +425,17 @@
                 rows = acc[:, where[0], where[1], :, pl.ds(0, UNITS)].reshape(64, UNITS)
                 hs[i2 * 64 : (i2 + 1) * 64, :] = rows.astype(jnp.bfloat16)
 
-        @pl.loop(0, WIDE // 256)
+        @pl.loop(0, WIDE // 512)
         def _(n):
-            cols = pl.ds(pl.multiple_of(part * WIDE + n * 256, 256), 256)
-            right = w_dn[:, :, :, cols].reshape(UNITS, 256)
+            cols = pl.ds(pl.multiple_of(part * WIDE + n * 512, 512), 512)
+            right = w_dn[:, :, :, cols].reshape(UNITS, 512)
             prod = jnp.dot(hs[0:total, :], right, preferred_element_type=jnp.float32)
-            cols = pl.ds(pl.multiple_of(n * 256, 256), 256)
+            cols = pl.ds(pl.multiple_of(n * 512, 512), 512)
             ref = toks[part]
             n2, n1 = ref.shape[1], ref.shape[2]
             for j, i3 in enumerate(slabs):
                 piece = prod[j * 128 : (j + 1) * 128] if part == 0 else prod
-                ref[i3, :, :, :, cols] = piece.reshape(n2, n1, ROWS, 256).astype(jnp.bfloat16)
+                ref[i3, :, :, :, cols] = piece.reshape(n2, n1, ROWS, 512).astype(jnp.bfloat16)
 
     rs_sends, (rs_order, _) = scatter_order()
 
@@ -467,7 +496,7 @@
             pltpu.VMEM((8, 4, 4, ROWS, 2 * UNITS), f32),
             pltpu.VMEM((8, 4, 4, ROWS, UNITS), f32),
             pltpu.VMEM((EXTRA, UNITS), bf16),
-            pltpu.VMEM((256, WIDE), bf16),
+            pltpu.VMEM((384, WIDE), bf16),
             pltpu.VMEM((256, UNITS), bf16),
             *lands,
             pltpu.SemaphoreType.DMA((6,)),

time: 138 us -> 125 us (0.906)
  Pallas kernels: 135 us -> 123 us
    pallas_call x1, Pallas kernels: 135 us -> 123 us  [local(): pl.pallas_call(kernel, out_shape=jax.ShapeDtypeStruct((ROWS, 3 * WIDE), b...]
where the time goes in v3:
time: 125 us; the launch traced here: 124 us
  Pallas kernels  123 us (98%)
  local copies, waits for them, and re-layouts  1.54 us (1%)
    pallas_call x1, Pallas kernels, local(): pl.pallas_call(kernel, out_shape=jax.ShapeDtypeStruct((ROWS, 3 * WIDE), b...  123 us

profile of v3, /device:TPU:8, one launch (start us, length us, event | category | flops | bytes accessed | tf_op | source)
XLA Modules:
  0.0 124.3 jit_solution(15859812958943538956)
XLA Ops:
  0.0 122.8 %expert_layer.1 = bf16[8,6144]{1,0:T(8,128)(2,1)} custom-call(bf16[8,6144]{1,0:T(8,128)(2,1)} %tok_ref.1, bf16[8,2,32,6144]{3,2,1,0:T(8,128)(2,1)} %gu_ref.1, bf16[8,32,6144]{2,1,0:T(8,128)(2,1)} %dn_ref.1, s32[2,8]{1,0:T(2,128)} %bitcast.2, f32[2,8]{1,0:T(2,128)} %bitcast.3, s32[8]{0:T(128)} %old_ref.1, s32[8]{0:T(128)} %new_ref.1), custom_call_target="tpu_custom_call" | custom-call | tf_op jit(solution)/shard_map/expert_layer/pallas_call | solution.py:485
  122.8 1.5 %copy.9 = bf16[8,6144]{1,0:T(8,128)(2,1)} copy(bf16[8,6144]{1,0:T(8,128)(2,1)} %expert_layer.1) | data formatting | bytes 196608

commit v4 on v3

--- a/solution.py
+++ b/solution.py
@@ -17,10 +17,26 @@
 UNITS = 2 * SLOTS * SLIVER
 RING = {"x": 4, "y": 4, "z": 8}
 ORDER = (("x", "y", "z"), ("z", "y", "x"), ("z", "x", "y"))
-RATE, LATENCY = 44500.0, 1.8
+RATE, LATENCY = 45500.0, 1.7
 AHEAD = 3.0
-GATHER_BONUS = {(2, 1): 2.1, (2, 2): 8.3, (1, 1): 12.7, (0, 2): 9.2, (0, 0): 12.6, (0, 1): -0.2, (1, 2): 11.2, (1, 0): 5.2, (2, 0): 5.8}
-SCATTER_BONUS = {(0, 0): -6.3, (2, 0): 13.8, (1, 0): 10.2, (1, 1): 9.9, (1, 2): -3.4, (0, 1): -1.4, (2, 1): -2.5, (0, 2): 5.3, (2, 2): -1.7}
+GATHER_BONUS = {
+    (0, 2, 1): 8.4, (2, 2, 1): -1.3, (1, 0, 1): 3.2, (2, 2, "i2", 0): 9.8, (2, 2, 2): -5.4,
+    (0, 2, "i2", 3): 7.1, (2, 2, "i2", 3): 3.1, (2, 1, 1): 1.3, (2, 2, "i2", 2): -0.2, (0, 1, 1): 9.9,
+    (1, 0, 3): 10.5, (1, 2, "i2", 0): -2.1, (2, 0): 13.6, (0, 2, 4): 2.1, (1, 1): 12.0,
+    (0, 2, "i2", 0): -1.6, (0, 2, 2): 12.4, (1, 2, "i2", 1): -0.8, (0, 0, 2): 13.3, (1, 2, 1): 1.1,
+    (1, 2, "i2", 2): -3.7, (1, 2, "i2", 3): -11.9, (0, 2, "i2", 1): 3.8, (0, 2): 9.5, (2, 0, 3): 13.3,
+    (1, 2): -12.6, (1, 1, 1): 2.7, (1, 2, 2): -9.8, (1, 0, 4): -6.2, (0, 1, 2): -0.8,
+    (1, 0, 2): -10.9, (2, 0, 4): -9.6, (2, 2, "i2", 1): 0.4, (1, 0): 0.1, (0, 2, "i2", 2): 12.3,
+    (0, 1): 6.0, (2, 2): -7.3, (2, 1): 11.6,
+}
+SCATTER_BONUS = {
+    (2, 2): -11.4, (0, 1): -5.1, (1, 0, 3): -1.7, (1, 0, 1): 6.8, (2, 2, "i2", 3): 7.5,
+    (0, 2, 2): -3.0, (2, 1): -1.0, (1, 2, "i2", 2): -1.4, (1, 2): -0.9, (1, 0, 4): 2.1,
+    (0, 1, 2): -1.5, (2, 2, 1): 3.3, (1, 1, 2): -10.2, (0, 2, 1): 3.3, (0, 2, "i2", 1): 8.6,
+    (1, 2, "i2", 0): -2.1, (2, 2, "i2", 2): -0.3, (1, 1, 1): -0.2, (2, 0, 2): 0.7, (2, 0, 4): -6.7,
+    (2, 0, 3): -6.4, (2, 0, 1): -9.0, (0, 0, 1): 2.7, (1, 2, "i2", 3): 1.5, (2, 0): 11.5,
+    (0, 2, 4): -7.1, (0, 0): -12.4, (0, 2, 3): -0.7,
+}
 
 
 class Message:
@@ -103,7 +119,10 @@
     now = 0.0
 
     def offer(key):
-        rank = tail(key) + (bonus or {}).get(key[:2], 0.0)
+        part, stage, dist, _, sub = key
+        extra = bonus or {}
+        i2 = subs_of(part, stage)[sub][0]
+        rank = tail(key) + sum(extra.get(k, 0.0) for k in ((part, stage), (part, stage, dist), (part, stage, "i2", i2)))
         heapq.heappush(queues.setdefault(sends[key][0].link, []), (-rank, number[key], key))
 
     def finish(token):
@@ -139,7 +158,7 @@
         job = next((j for j in jobs if j[2] <= done), None)
         if pick is not None:
             ready.remove(pick)
-            now += recv_cost
+            now += recv_cost(sends[pick[1]])
             order.append(("recv", pick[1]))
             finish(("recv",) + pick[1])
             handled += 1
@@ -172,38 +191,36 @@
     for part, slabs, i2s, held in GATE_UP_JOBS:
         needs = {v for k, v in source.items() if k[0] == part and k[1] in slabs and k[2] in i2s}
         rows = (32 if part == 0 else 64) * len(i2s) * len(slabs)
-        cost = UP_COST[rows] * len(held)
+        cost = PREPARE_COST * rows + UP_COST[rows] * len(held)
         jobs.append((("up", part, slabs, i2s, held), cost, needs | {("weights", held[-1])}))
     timers = [(OWN_AT, ("weights", 0)), (PARTNER_AT, ("weights", 1))]
-    return sends, simulate(sends, {m.key: set() for m in msgs}, jobs, 0.1, timers, bonus=GATHER_BONUS)
+    return sends, simulate(sends, {m.key: set() for m in msgs}, jobs, lambda s: 0.05, timers, bonus=GATHER_BONUS)
 
 
 OWN_AT, PARTNER_AT = 5.0, 20.0
-UP_COST = {64: 0.75, 128: 0.8, 192: 0.85, 256: 0.9, 384: 1.3}
+PREPARE_COST = 0.0008
+UP_COST = {64: 0.65, 128: 0.67, 192: 0.7, 256: 0.76, 384: 1.08}
 HIDDEN_COST = (0.8, 0.4, 0.7, 1.5)
 ALL = (0, 1, 2, 3)
 GATE_UP_JOBS = (
+    (2, (1,), ALL, (0, 1)),
+    (1, (0,), ALL, (0, 1)),
+    (2, (3,), (0,), (0, 1)),
+    (0, (3, 4), ALL, (0, 1)),
+    (2, (3,), (1, 2, 3), (0, 1)),
+    (0, (7,), ALL, (0, 1)),
+    (2, (0,), ALL, (0, 1)),
+    (1, (1,), ALL, (0, 1)),
+    (0, (5, 6), ALL, (0, 1)),
+    (2, (2,), ALL, (0, 1)),
+    (0, (0, 1, 2), ALL, (0, 1)),
+    (1, (2,), ALL, (0, 1)),
     (1, (3,), ALL, (0, 1)),
-    (1, (1,), (0,), (0, 1)),
-    (0, (7,), ALL, (0, 1)),
-    (0, (0, 1, 2), ALL, (0, 1)),
-    (1, (2,), (1, 2, 3), (0, 1)),
-    (1, (2,), (0,), (0, 1)),
-    (2, (0,), ALL, (0, 1)),
-    (1, (0,), (2, 3), (0, 1)),
-    (2, (2,), ALL, (0, 1)),
-    (1, (0,), (0, 1), (0, 1)),
-    (2, (1,), (0, 1), (0, 1)),
-    (2, (1,), (2, 3), (0, 1)),
-    (2, (3,), ALL, (0, 1)),
-    (1, (1,), (1, 2, 3), (0, 1)),
-    (0, (3, 4), ALL, (0, 1)),
-    (0, (5, 6), ALL, (0, 1)),
 )
 DOWN_JOBS = (
     ("hid", 0), (2, (3,)), ("hid", 1), (0, (7,)), ("hid", 2), (1, (3,)),
     ("hid", 3), (0, (5, 6)), (1, (1,)), (2, (1,)), (2, (2,)), (0, (3, 4)),
-    (1, (2,)), (2, (0,)), (0, (0,)), (1, (0,)), (0, (1, 2)),
+    (1, (2,)), (2, (0,)), (0, (1, 2)), (1, (0,)), (0, (0,)),
 )
 
 
@@ -235,7 +252,7 @@
             jobs.append((("hid", slabs), HIDDEN_COST[slabs], set()))
         else:
             jobs.append((("down", part, slabs), 0.75 * len(slabs) if part == 0 else 1.1, set()))
-    return sends, simulate(sends, recv_needs, jobs, 0.2, bonus=SCATTER_BONUS)
+    return sends, simulate(sends, recv_needs, jobs, lambda s: 0.04 + s[1] * 0.8e-6, bonus=SCATTER_BONUS)
 
 
 def device_at(x, y, z, core):
@@ -244,10 +261,10 @@
 
 
 def kernel(
-    tok_ref, gu_ref, dn_ref, ids_ref, gv_ref, old_ref, new_ref, out_ref,
+    tok_ref, gu_ref, dn_ref, ids_hbm, gv_hbm, old_hbm, new_hbm, out_ref,
     tok0, tok1, tok2, w_gu, w_dn, acc, scale, spread, xs, hs,
     l30, l20, l10, l31, l21, l11, l32, l22, l12,
-    own_sem, w_send, w_recv, ag_send, ag_recv, rs_send, rs_recv,
+    ids_ref, gv_ref, old_ref, new_ref, table_sem, own_sem, w_send, w_recv, ag_send, ag_recv, rs_send, rs_recv,
 ):
     toks = (tok0, tok1, tok2)
     lands = ((l10, l20, l30), (l11, l21, l31), (l12, l22, l32))
@@ -264,6 +281,12 @@
     for dev in (partner, *near.values()):
         pl.semaphore_signal(barrier, inc=1, device_id=dev, device_id_type=mesh_id)
 
+    tables = [
+        pltpu.make_async_copy(src, dst, table_sem.at[i])
+        for i, (src, dst) in enumerate(((ids_hbm, ids_ref), (gv_hbm, gv_ref), (old_hbm, old_ref), (new_hbm, new_ref)))
+    ]
+    for copy in tables:
+        copy.start()
     own = [
         pltpu.make_async_copy(tok_ref.at[:, pl.ds(p * WIDE, WIDE)], toks[p].at[0, 0, 0, :, pl.ds(0, WIDE)], own_sem.at[p])
         for p in range(3)
@@ -277,6 +300,9 @@
     ]
     for copy in own_w:
         copy.start()
+
+    for copy in tables:
+        copy.wait()
 
     lane = lax.broadcasted_iota(jnp.int32, (ROWS, EXTRA), 1)
     slot = lax.rem(lane, SLOTS)
@@ -301,8 +327,7 @@
     coded = jnp.where(lane < SLOTS, high, jnp.where(lane < 2 * SLOTS, weight - high, 0.0))
     tok0[0, 0, 0, :, WIDE:] = coded.astype(jnp.bfloat16)
 
-    for copy in own:
-        copy.wait()
+    own[0].wait()
     pl.semaphore_wait(barrier, 7)
 
     def remote(src, dst, send, recv, dev):
@@ -322,8 +347,11 @@
     index = {key: i for i, key in enumerate(ag_sends)}
     gathers = {}
     for key, (m, _, _) in ag_sends.items():
+        source, target = view(m, -(m.dist - 1) * m.sign, False), view(m, -m.dist * m.sign, False)
+        if m.part and blocks_of(m, -(m.dist - 1) * m.sign) == [(0, 0, 0)]:
+            source, target = tok_ref.at[:, pl.ds(m.part * WIDE, WIDE)], target.at[0]
         gathers[key] = remote(
-            view(m, -(m.dist - 1) * m.sign, False), view(m, -m.dist * m.sign, False),
+            source, target,
             ag_send.at[index[key]], ag_recv.at[index[key]], near[m.link],
         )
     crossing = [
@@ -386,7 +414,7 @@
             for copy in crossing:
                 copy.wait()
         elif what == ("weights", 0):
-            for copy in own_w:
+            for copy in own[1:] + own_w:
                 copy.wait()
         else:
             gate_up(*what[1:])
@@ -474,7 +502,6 @@
     bf16, f32 = jnp.bfloat16, jnp.float32
     any_space = pl.BlockSpec(memory_space=pl.ANY)
     vmem = pl.BlockSpec(memory_space=pltpu.VMEM)
-    smem = pl.BlockSpec(memory_space=pltpu.SMEM)
     lands = []
     for part in range(3):
         for stage in (2, 1, 0):
@@ -485,7 +512,7 @@
     return pl.pallas_call(
         kernel,
         out_shape=jax.ShapeDtypeStruct((ROWS, 3 * WIDE), bf16),
-        in_specs=[any_space, any_space, any_space, vmem, vmem, smem, smem],
+        in_specs=[any_space] * 7,
         out_specs=vmem,
         scratch_shapes=[
             pltpu.VMEM((8, 4, 4, ROWS, WIDE + EXTRA), bf16),
@@ -499,6 +526,11 @@
             pltpu.VMEM((384, WIDE), bf16),
             pltpu.VMEM((256, UNITS), bf16),
             *lands,
+            pltpu.VMEM((2, ROWS), jnp.int32),
+            pltpu.VMEM((2, ROWS), f32),
+            pltpu.SMEM((SLOTS,), jnp.int32),
+            pltpu.SMEM((SLOTS,), jnp.int32),
+            pltpu.SemaphoreType.DMA((4,)),
             pltpu.SemaphoreType.DMA((6,)),
             pltpu.SemaphoreType.DMA((3,)),
             pltpu.SemaphoreType.DMA((3,)),

time: 125 us -> 123 us (0.984)
  Pallas kernels: 123 us -> 121 us
    pallas_call x1, Pallas kernels: 123 us -> 121 us  [local(): pl.pallas_call(kernel, out_shape=jax.ShapeDtypeStruct((ROWS, 3 * WIDE), b...]
where the time goes in v4:
time: 123 us
  Pallas kernels  121 us (98%)
  local copies, waits for them, and re-layouts  1.54 us (1%)
    pallas_call x1, Pallas kernels, local(): pl.pallas_call(kernel, out_shape=jax.ShapeDtypeStruct((ROWS, 3 * WIDE), b...  121 us

profile of v4, /device:TPU:8, one launch (start us, length us, event | category | flops | bytes accessed | tf_op | source)
XLA Modules:
  0.0 122.7 jit_solution(4840140388670569489)
XLA Ops:
  0.0 121.2 %expert_layer.1 = bf16[8,6144]{1,0:T(8,128)(2,1)} custom-call(bf16[8,6144]{1,0:T(8,128)(2,1)} %tok_ref.1, bf16[8,2,32,6144]{3,2,1,0:T(8,128)(2,1)} %gu_ref.1, bf16[8,32,6144]{2,1,0:T(8,128)(2,1)} %dn_ref.1, s32[2,8]{1,0:T(2,128)} %bitcast.2, f32[2,8]{1,0:T(2,128)} %bitcast.3, s32[8]{0:T(128)} %old_hbm.1, s32[8]{0:T(128)} %new_hbm.1), custom_call_target="tpu_custom_call" | custom-call | tf_op jit(solution)/shard_map/expert_layer/pallas_call | solution.py:512
  121.2 1.5 %copy.9 = bf16[8,6144]{1,0:T(8,128)(2,1)} copy(bf16[8,6144]{1,0:T(8,128)(2,1)} %expert_layer.1) | data formatting | bytes 196608

commit v5 on v4

--- a/solution.py
+++ b/solution.py
@@ -198,7 +198,7 @@
 
 
 OWN_AT, PARTNER_AT = 5.0, 20.0
-PREPARE_COST = 0.0008
+PREPARE_COST = 0.0001
 UP_COST = {64: 0.65, 128: 0.67, 192: 0.7, 256: 0.76, 384: 1.08}
 HIDDEN_COST = (0.8, 0.4, 0.7, 1.5)
 ALL = (0, 1, 2, 3)
@@ -262,7 +262,7 @@
 
 def kernel(
     tok_ref, gu_ref, dn_ref, ids_hbm, gv_hbm, old_hbm, new_hbm, out_ref,
-    tok0, tok1, tok2, w_gu, w_dn, acc, scale, spread, xs, hs,
+    tok0, tok1, tok2, w_gu, w_dn, acc, scale, spread, hs,
     l30, l20, l10, l31, l21, l11, l32, l22, l12,
     ids_ref, gv_ref, old_ref, new_ref, table_sem, own_sem, w_send, w_recv, ag_send, ag_recv, rs_send, rs_recv,
 ):
@@ -362,23 +362,15 @@
 
     def gate_up(part, slabs, i2s, held):
         ref = toks[part]
-        count, rows = len(i2s), ref.shape[2] * ROWS
-        step = i2s[1] - i2s[0] if count > 1 else 1
-        for j, i3 in enumerate(slabs):
-
-            @pl.loop(0, count)
-            def _(i2):
-                block = ref[i3, i2s[0] + step * i2, :, :, pl.ds(0, WIDE)].astype(jnp.float32)
-                start = pl.multiple_of((j * count + i2) * rows, 16)
-                xs[pl.ds(start, rows), :] = block.reshape(rows, WIDE).astype(jnp.bfloat16)
-
-        total = count * rows * len(slabs)
+        count = len(i2s)
+        total = len(slabs) * count * ref.shape[2] * ROWS
 
         @pl.loop(held[0], held[-1] + 1)
         def _(group):
             right = w_gu[group, :, :, :, pl.ds(part * WIDE, WIDE)].reshape(UNITS, WIDE)
+            left = ref[pl.ds(slabs[0], len(slabs)), pl.ds(i2s[0], count), :, :, pl.ds(0, WIDE)].reshape(total, WIDE)
             prod = lax.dot_general(
-                xs[0:total, :], right, (((1,), (1,)), ((), ())), preferred_element_type=jnp.float32
+                left, right, (((1,), (1,)), ((), ())), preferred_element_type=jnp.float32
             )
             cols = pl.ds(pl.multiple_of(group * UNITS, UNITS), UNITS)
             if part == 0:
@@ -523,7 +515,6 @@
             pltpu.VMEM((8, 4, 4, ROWS, 2 * UNITS), f32),
             pltpu.VMEM((8, 4, 4, ROWS, UNITS), f32),
             pltpu.VMEM((EXTRA, UNITS), bf16),
-            pltpu.VMEM((384, WIDE), bf16),
             pltpu.VMEM((256, UNITS), bf16),
             *lands,
             pltpu.VMEM((2, ROWS), jnp.int32),

time: 123 us -> 123 us (level)
  no operation moved by 1% of the time
where the time goes in v5:
time: 123 us
  Pallas kernels  121 us (98%)
  local copies, waits for them, and re-layouts  1.54 us (1%)
    pallas_call x1, Pallas kernels, local(): pl.pallas_call(kernel, out_shape=jax.ShapeDtypeStruct((ROWS, 3 * WIDE), b...  121 us

profile of v5, /device:TPU:8, one launch (start us, length us, event | category | flops | bytes accessed | tf_op | source)
XLA Modules:
  0.0 122.5 jit_solution(7819061049423504846)
XLA Ops:
  0.0 121.0 %expert_layer.1 = bf16[8,6144]{1,0:T(8,128)(2,1)} custom-call(bf16[8,6144]{1,0:T(8,128)(2,1)} %tok_ref.1, bf16[8,2,32,6144]{3,2,1,0:T(8,128)(2,1)} %gu_ref.1, bf16[8,32,6144]{2,1,0:T(8,128)(2,1)} %dn_ref.1, s32[2,8]{1,0:T(2,128)} %bitcast.2, f32[2,8]{1,0:T(2,128)} %bitcast.3, s32[8]{0:T(128)} %old_hbm.1, s32[8]{0:T(128)} %new_hbm.1), custom_call_target="tpu_custom_call" | custom-call | tf_op jit(solution)/shard_map/expert_layer/pallas_call | solution.py:504
  121.0 1.5 %copy.9 = bf16[8,6144]{1,0:T(8,128)(2,1)} copy(bf16[8,6144]{1,0:T(8,128)(2,1)} %expert_layer.1) | data formatting | bytes 196608

commit v6 on v5

--- a/solution.py
+++ b/solution.py
@@ -469,6 +469,11 @@
             view(m, m.dist * m.sign, True), landing(m),
             rs_send.at[index[key]], rs_recv.at[index[key]], near[m.link],
         )
+    results = [
+        pltpu.make_async_copy(toks[p].at[0, 0, 0, :, pl.ds(0, WIDE)], out_ref.at[:, pl.ds(p * WIDE, WIDE)], own_sem.at[p])
+        for p in range(3)
+    ]
+    left = [sum(key[0] == p for key in rs_sends) for p in range(3)]
     for kind, what in rs_order:
         if kind == "send":
             scatters[what].start()
@@ -481,8 +486,11 @@
             scatters[what].wait_recv()
             target = view(m, (m.dist - 1) * m.sign, True)
             target[...] = target[...] + landing(m)[...]
-    for p in range(3):
-        out_ref[:, p * WIDE : (p + 1) * WIDE] = toks[p][0, 0, 0, :, 0:WIDE]
+            left[m.part] -= 1
+            if not left[m.part]:
+                results[m.part].start()
+    for copy in results:
+        copy.wait()
     for copy in scatters.values():
         copy.wait_send()
 
@@ -493,7 +501,6 @@
     count = len(messages())
     bf16, f32 = jnp.bfloat16, jnp.float32
     any_space = pl.BlockSpec(memory_space=pl.ANY)
-    vmem = pl.BlockSpec(memory_space=pltpu.VMEM)
     lands = []
     for part in range(3):
         for stage in (2, 1, 0):
@@ -505,7 +512,7 @@
         kernel,
         out_shape=jax.ShapeDtypeStruct((ROWS, 3 * WIDE), bf16),
         in_specs=[any_space] * 7,
-        out_specs=vmem,
+        out_specs=any_space,
         scratch_shapes=[
             pltpu.VMEM((8, 4, 4, ROWS, WIDE + EXTRA), bf16),
             pltpu.VMEM((4, 4, 8, ROWS, WIDE), bf16),

time: 123 us -> 123 us (level)
  no operation moved by 1% of the time
where the time goes in v6:
time: 123 us; the launch traced here: 122 us
  Pallas kernels  121 us (98%)
  local copies, waits for them, and re-layouts  1.54 us (1%)
    pallas_call x1, Pallas kernels, local(): pl.pallas_call(kernel, out_shape=jax.ShapeDtypeStruct((ROWS, 3 * WIDE), b...  121 us

profile of v6, /device:TPU:8, one launch (start us, length us, event | category | flops | bytes accessed | tf_op | source)
XLA Modules:
  0.0 122.5 jit_solution(7085379505596302409)
XLA Ops:
  0.0 120.9 %expert_layer.1 = bf16[8,6144]{1,0:T(8,128)(2,1)} custom-call(bf16[8,6144]{1,0:T(8,128)(2,1)} %tok_ref.1, bf16[8,2,32,6144]{3,2,1,0:T(8,128)(2,1)} %gu_ref.1, bf16[8,32,6144]{2,1,0:T(8,128)(2,1)} %dn_ref.1, s32[2,8]{1,0:T(2,128)} %bitcast.2, f32[2,8]{1,0:T(2,128)} %bitcast.3, s32[8]{0:T(128)} %old_hbm.1, s32[8]{0:T(128)} %new_hbm.1), custom_call_target="tpu_custom_call" | custom-call | tf_op jit(solution)/shard_map/expert_layer/pallas_call | solution.py:511
  120.9 1.5 %copy.9 = bf16[8,6144]{1,0:T(8,128)(2,1)} copy(bf16[8,6144]{1,0:T(8,128)(2,1)} %expert_layer.1) | data formatting | bytes 196608
